TPU v7x, 128 devices: a whole 4x4x4 slice. The times are simulated.
128 devices in a mesh: cells: 64 (over z, x_hi, y, core), waves: 2 (over x_lo).
Axes of the slice: x: 4 (x_hi: 2, x_lo: 2; x = x_hi * 2 + x_lo), y: 4, z: 4, core: 2. Of those that a mesh axis runs over, the one named last changes fastest.
Arguments:
- features: bfloat16 [131072, 512], P('cells', 'waves'), may hold values from -6 to 6
- positions: float32 [3, 131072], P(None, 'cells'), may hold values from 0 to 1024, as said below
- occupancy: int32 [1024], P('cells'), may hold values from 1 to 128, as said below
- neighbours: int32 [1024, 3], P('cells'), may hold values from -2 to 2, as said below
- wavevectors: float32 [3, 4096], P(None, 'waves'), may hold values from -1 to 1
- filters: float32 [4096, 512], P('waves'), may hold values from -6 to 6
- falloffs: float32 [4], replicated, may hold values from 0.05 to 2
- mixing: float32 [4, 512], replicated, may hold values from -2 to 2
- norm_gain: float32 [512], replicated, may hold values from 0.5 to 1.5
- in_weight: bfloat16 [512, 1024], P(None, 'waves'), may hold values from -0.25 to 0.25
- out_weight: bfloat16 [1024, 512], P('waves'), may hold values from -0.1875 to 0.1875
Outputs:
- result: bfloat16 [131072, 512], P('cells', 'waves')
Inputs may be any that keep to these rules, and one draw needn't show every extreme that they name: `occupancy`: the atoms of a cell fill its first slots; the last cell is full. `neighbours`: each row holds 3 distinct offsets; cell c interacts with cells c + offset modulo 1024. `positions`: the first coordinate of an atom in cell c lies in [c, c + 1]; the other two lie in [0, 3].
All inputs are finite; a program needn't handle non-finite values.
Results may differ from a plain program's by a relative error of at most 0.009.
Values may be sent and summed in bfloat16 or wider, within the bound.
A program may use at most 128 MiB of HBM per device.

v0:
```python
import math

import jax
import jax.numpy as jnp
from jax import lax
from jax.sharding import PartitionSpec as P

K = 4096
HW = 2


EPS = 1e-06


def extended(cells, sides, width):
    for axis, dim in sides:
        count = lax.axis_size(axis)
        head = lax.slice_in_dim(cells, 0, width, axis=dim)
        tail = lax.slice_in_dim(cells, cells.shape[dim] - width, cells.shape[dim], axis=dim)
        cells = jnp.concatenate(
            [
                lax.ppermute(tail, axis, [(i, (i + 1) % count) for i in range(count)]),
                cells,
                lax.ppermute(head, axis, [((i + 1) % count, i) for i in range(count)]),
            ],
            axis=dim,
        )
    return cells


def wrap_long(along_x, length):
    return jnp.where(
        along_x > 0.5 * length,
        along_x - length,
        jnp.where(along_x < -0.5 * length, along_x + length, along_x),
    )


def phases_of(block_waves, positions):
    return (
        block_waves[0][:, None] * positions[0][None, :]
        + block_waves[1][:, None] * positions[1][None, :]
        + block_waves[2][:, None] * positions[2][None, :]
    )


def trig_blocks(block_waves, positions):
    phases = phases_of(block_waves, positions)
    return (jnp.cos(phases).astype(jnp.bfloat16), jnp.sin(phases).astype(jnp.bfloat16))


def near_messages(wide_feats, wide_pos, cell_pos, neighbours, falloffs, coefs, length):
    cell_count = cell_pos.shape[0]
    partner_rows = jnp.arange(cell_count, dtype=jnp.int32)[:, None] + HW + neighbours
    partner_pos = wide_pos[partner_rows]
    partner_feats = wide_feats[partner_rows]
    displace = cell_pos[:, None, :, :, None] - partner_pos[:, :, :, None, :]
    along_x = wrap_long(displace[:, :, 0], length)
    squared = (
        along_x * along_x
        + displace[:, :, 1] * displace[:, :, 1]
        + displace[:, :, 2] * displace[:, :, 2]
    )
    kernel = jnp.exp(-falloffs[:, None, None, None, None] * squared[None]).astype(jnp.bfloat16)
    messages = jnp.einsum(
        "gcnij,cnjf->gcif", kernel, partner_feats, preferred_element_type=jnp.float32
    )
    near = jnp.sum(messages * coefs[:, None, None, :], axis=0)
    return near.reshape(cell_count * cell_pos.shape[2], coefs.shape[1])


def shards(
    features,
    positions,
    occupancy,
    neighbours,
    wavevectors,
    filters,
    falloffs,
    mixing,
    norm_gain,
    in_weight,
    out_weight,
):
    cell_count = occupancy.shape[0]
    atom_rows = features.shape[0]
    capacity = atom_rows // cell_count
    part_width = features.shape[1]
    full_width = mixing.shape[1]
    length = jnp.float32(lax.axis_size("cells") * cell_count)
    count = lax.psum(jnp.sum(occupancy).astype(jnp.float32), "cells")
    is_live = (jnp.arange(capacity, dtype=jnp.int32)[None, :] < occupancy[:, None]).reshape(
        atom_rows, 1
    )
    whole = lax.all_gather(features, "waves", axis=1, tiled=True)
    masked_whole = jnp.where(is_live, whole, jnp.zeros_like(whole))
    cell_pos = positions.reshape(3, cell_count, capacity).transpose(1, 0, 2)
    wide_pos = extended(cell_pos, (("cells", 0),), HW)
    wave_rows = wavevectors.shape[1]
    block_rows = math.gcd(wave_rows, 512)
    stacked = wavevectors.reshape(3, wave_rows // block_rows, block_rows).transpose(1, 0, 2)

    def forward(block_waves):
        cosine_block, sine_block = trig_blocks(block_waves, positions)
        return (
            jnp.dot(cosine_block, masked_whole, preferred_element_type=jnp.float32),
            jnp.dot(sine_block, masked_whole, preferred_element_type=jnp.float32),
        )

    cos_sum, sin_sum = lax.map(forward, stacked)
    cos_sum = cos_sum.reshape(wave_rows, full_width)
    sin_sum = sin_sum.reshape(wave_rows, full_width)
    empty = jnp.zeros((atom_rows, full_width), jnp.float32)
    count_root = jnp.sqrt(count)
    cos_total, sin_total = lax.psum((cos_sum, sin_sum), "cells")
    cos_filtered = (filters * (cos_total / count_root)).astype(jnp.bfloat16)
    sin_filtered = (filters * (sin_total / count_root)).astype(jnp.bfloat16)
    piece_rows = cos_filtered.shape[0]
    inner_rows = math.gcd(piece_rows, 512)
    contract = (((0,), (0,)), ((), ()))

    def add_block(block_number, total_far):
        begin = block_number * inner_rows
        block_waves = lax.dynamic_slice_in_dim(wavevectors, 0 + begin, inner_rows, 1)
        cosine_block, sine_block = trig_blocks(block_waves, positions)
        cos_part = lax.dynamic_slice_in_dim(cos_filtered, begin, inner_rows, 0)
        sin_part = lax.dynamic_slice_in_dim(sin_filtered, begin, inner_rows, 0)
        total_far = total_far + lax.dot_general(
            cosine_block, cos_part, contract, preferred_element_type=jnp.float32
        )
        return total_far + lax.dot_general(
            sine_block, sin_part, contract, preferred_element_type=jnp.float32
        )

    far_sum = lax.fori_loop(0, piece_rows // inner_rows, add_block, empty)
    column = lax.axis_index("waves") * part_width
    masked_part = jnp.where(is_live, features, jnp.zeros_like(features))
    wide_feats = extended(
        masked_part.reshape(cell_count, capacity, part_width), (("cells", 0),), HW
    )
    coefs = lax.dynamic_slice_in_dim(mixing, column, part_width, 1)
    near = near_messages(wide_feats, wide_pos, cell_pos, neighbours, falloffs, coefs, length)
    far_part = lax.psum_scatter(
        far_sum.astype(jnp.bfloat16), "waves", scatter_dimension=1, tiled=True
    ).astype(jnp.float32) / math.sqrt(K)
    merged_part = features.astype(jnp.float32) + near + far_part
    merged = lax.all_gather(merged_part.astype(jnp.bfloat16), "waves", axis=1, tiled=True).astype(
        merged_part.dtype
    )
    normed = (
        merged * lax.rsqrt(jnp.mean(merged * merged, axis=-1, keepdims=True) + EPS) * norm_gain
    ).astype(jnp.bfloat16)
    hidden = jax.nn.silu(jnp.dot(normed, in_weight, preferred_element_type=jnp.float32)).astype(
        jnp.bfloat16
    )
    mlp_terms = jnp.dot(hidden, out_weight, preferred_element_type=jnp.float32)
    mlp_part = lax.psum_scatter(
        mlp_terms.astype(jnp.bfloat16), "waves", scatter_dimension=1, tiled=True
    ).astype(jnp.float32)
    return (merged_part + mlp_part).astype(jnp.bfloat16)


def solution(mesh):
    placed = (
        P("cells", "waves"),
        P(None, "cells"),
        P("cells"),
        P("cells", None),
        P(None, "waves"),
        P("waves", None),
        P(),
        P(),
        P(),
        P(None, "waves"),
        P("waves", None),
    )
    return jax.shard_map(
        shards, mesh=mesh, in_specs=placed, out_specs=P("cells", "waves"), check_vma=False
    )
```

profile of v0, /device:TPU:1, one launch (start us, length us, event | category | flops | bytes accessed | tf_op | source)
XLA Modules:
  0.0 1142.6 jit_solution(7534821904349810831)
XLA Ops:
  6.5 0.7 all-gather.3.cloned.1.call-update
  7.3 0.0 all-reduce.3.cloned.1.call-start
  7.3 0.7 fusion.59
  8.1 39.8 %all-gather.3.cloned.1.call-done = bf16[2048,512]{1,0:T(8,128)(2,1)} async-done(((bf16[2048,256]{1,0:T(8,128)(2,1)}), bf16[2048,512]{1,0:T(8,128)(2,1)}) %all-gather.3.cloned.1.call-update) | async-done | bytes 2097168 | tf_op jit(solution)/shard_map/all_gather | solution.py:95
  47.8 1.8 broadcast_select_fusion
  49.6 125.5 %while.26 = (s32[]{:T(128)}, f32[4,512,512]{2,1,0:T(8,128)}, f32[4,512,512]{2,1,0:T(8,128)}, f32[4,3,512]{2,1,0:T(4,128)}, f32[3,2048]{1,0:T(4,128)S(1)}, /*inde...) while((s32[]{:T(128)}, f32[4,512,512]{2,1,0:T(8,128)}, f32[4,512,512]{2,1,0:T(8,128)}, ...), condition=%wide.region_2.3_spmd, body=%wide.region_1.0_spmd.sunk | while | flops 2160066560 | bytes 6415497 | solution.py:110
  49.6 0.8 constant_dynamic-slice_fusion.7
  50.5 15.4 %fusion.84 = f32[4,512,512]{2,1,0:T(8,128)} fusion(f32[4,512,512]{2,1,0:T(8,128)} %get-tuple-element.325, s32[]{:T(128)} %get-tuple-element.323, bf16[2048,512]{1,0:T(8,128)(2,1)S(1)} %get-tuple-element.338, f32[2048]{0:T(1024)S(1)} %bitcast.119, f32[512]{0:T(512)S(1)} %bitcast.137, f32[2048]{0:T(1024)S(1)} %bitcast.121, f32[512]{0:T(512)S(1)} %bitcast.135, ...), kind=kOutput, calls=%fused_computation.20.clone.1 | convolution fusion | flops 1080033280 | bytes 3176960 | tf_op jit(solution)/shard_map/while/body/eval_jaxpr/dot_general | solution.py:107
  65.8 15.2 %fusion.83 = f32[4,512,512]{2,1,0:T(8,128)} fusion(f32[4,512,512]{2,1,0:T(8,128)} %get-tuple-element.324, s32[]{:T(128)} %get-tuple-element.323, bf16[2048,512]{1,0:T(8,128)(2,1)S(1)} %get-tuple-element.338, f32[2048]{0:T(1024)S(1)} %bitcast.120, f32[512]{0:T(512)S(1)} %bitcast.138, f32[2048]{0:T(1024)S(1)} %bitcast.122, f32[512]{0:T(512)S(1)} %bitcast.136, ...), kind=kOutput, calls=%fused_computation.22.clone.1 | convolution fusion | flops 1080033280 | bytes 3176960 | tf_op jit(solution)/shard_map/while/body/eval_jaxpr/dot_general | solution.py:106
  81.0 0.8 constant_dynamic-slice_fusion.7
  81.8 15.4 %fusion.84 = f32[4,512,512]{2,1,0:T(8,128)} fusion(f32[4,512,512]{2,1,0:T(8,128)} %get-tuple-element.325, s32[]{:T(128)} %get-tuple-element.323, bf16[2048,512]{1,0:T(8,128)(2,1)S(1)} %get-tuple-element.338, f32[2048]{0:T(1024)S(1)} %bitcast.119, f32[512]{0:T(512)S(1)} %bitcast.137, f32[2048]{0:T(1024)S(1)} %bitcast.121, f32[512]{0:T(512)S(1)} %bitcast.135, ...), kind=kOutput, calls=%fused_computation.20.clone.1 | convolution fusion | flops 1080033280 | bytes 3176960 | tf_op jit(solution)/shard_map/while/body/eval_jaxpr/dot_general | solution.py:107
  97.2 15.2 %fusion.83 = f32[4,512,512]{2,1,0:T(8,128)} fusion(f32[4,512,512]{2,1,0:T(8,128)} %get-tuple-element.324, s32[]{:T(128)} %get-tuple-element.323, bf16[2048,512]{1,0:T(8,128)(2,1)S(1)} %get-tuple-element.338, f32[2048]{0:T(1024)S(1)} %bitcast.120, f32[512]{0:T(512)S(1)} %bitcast.138, f32[2048]{0:T(1024)S(1)} %bitcast.122, f32[512]{0:T(512)S(1)} %bitcast.136, ...), kind=kOutput, calls=%fused_computation.22.clone.1 | convolution fusion | flops 1080033280 | bytes 3176960 | tf_op jit(solution)/shard_map/while/body/eval_jaxpr/dot_general | solution.py:106
  112.4 0.8 constant_dynamic-slice_fusion.7
  113.2 15.3 %fusion.84 = f32[4,512,512]{2,1,0:T(8,128)} fusion(f32[4,512,512]{2,1,0:T(8,128)} %get-tuple-element.325, s32[]{:T(128)} %get-tuple-element.323, bf16[2048,512]{1,0:T(8,128)(2,1)S(1)} %get-tuple-element.338, f32[2048]{0:T(1024)S(1)} %bitcast.119, f32[512]{0:T(512)S(1)} %bitcast.137, f32[2048]{0:T(1024)S(1)} %bitcast.121, f32[512]{0:T(512)S(1)} %bitcast.135, ...), kind=kOutput, calls=%fused_computation.20.clone.1 | convolution fusion | flops 1080033280 | bytes 3176960 | tf_op jit(solution)/shard_map/while/body/eval_jaxpr/dot_general | solution.py:107
  128.5 15.2 %fusion.83 = f32[4,512,512]{2,1,0:T(8,128)} fusion(f32[4,512,512]{2,1,0:T(8,128)} %get-tuple-element.324, s32[]{:T(128)} %get-tuple-element.323, bf16[2048,512]{1,0:T(8,128)(2,1)S(1)} %get-tuple-element.338, f32[2048]{0:T(1024)S(1)} %bitcast.120, f32[512]{0:T(512)S(1)} %bitcast.138, f32[2048]{0:T(1024)S(1)} %bitcast.122, f32[512]{0:T(512)S(1)} %bitcast.136, ...), kind=kOutput, calls=%fused_computation.22.clone.1 | convolution fusion | flops 1080033280 | bytes 3176960 | tf_op jit(solution)/shard_map/while/body/eval_jaxpr/dot_general | solution.py:106
  143.7 0.8 constant_dynamic-slice_fusion.7
  144.6 15.3 %fusion.84 = f32[4,512,512]{2,1,0:T(8,128)} fusion(f32[4,512,512]{2,1,0:T(8,128)} %get-tuple-element.325, s32[]{:T(128)} %get-tuple-element.323, bf16[2048,512]{1,0:T(8,128)(2,1)S(1)} %get-tuple-element.338, f32[2048]{0:T(1024)S(1)} %bitcast.119, f32[512]{0:T(512)S(1)} %bitcast.137, f32[2048]{0:T(1024)S(1)} %bitcast.121, f32[512]{0:T(512)S(1)} %bitcast.135, ...), kind=kOutput, calls=%fused_computation.20.clone.1 | convolution fusion | flops 1080033280 | bytes 3176960 | tf_op jit(solution)/shard_map/while/body/eval_jaxpr/dot_general | solution.py:107
  159.9 15.2 %fusion.83 = f32[4,512,512]{2,1,0:T(8,128)} fusion(f32[4,512,512]{2,1,0:T(8,128)} %get-tuple-element.324, s32[]{:T(128)} %get-tuple-element.323, bf16[2048,512]{1,0:T(8,128)(2,1)S(1)} %get-tuple-element.338, f32[2048]{0:T(1024)S(1)} %bitcast.120, f32[512]{0:T(512)S(1)} %bitcast.138, f32[2048]{0:T(1024)S(1)} %bitcast.122, f32[512]{0:T(512)S(1)} %bitcast.136, ...), kind=kOutput, calls=%fused_computation.22.clone.1 | convolution fusion | flops 1080033280 | bytes 3176960 | tf_op jit(solution)/shard_map/while/body/eval_jaxpr/dot_general | solution.py:106
  175.1 0.0 all-reduce.3.cloned.1.call-update
  175.1 0.0 reduce-scatter.3.cloned.1.call-start
  175.2 0.6 copy-done.5
  175.7 0.6 reduce_sum.28
  177.0 163.1 %psum.22 = f32[]{:T(128)} all-reduce(f32[]{:T(128)S(6)} %convert_element_type.64), channel_id=1, replica_groups=mesh['cells'=64,'waves'=2] {'cells'}, use_global_device_ids=true, to_apply=%region_5.6 | all-reduce | flops 1 | bytes 8 | tf_op jit(solution)/shard_map/psum | solution.py:91
  340.8 496.8 %all-reduce.3.cloned.1.call-done = (f32[2048,512]{1,0:T(8,128)}, f32[2048,512]{1,0:T(8,128)}) async-done(((f32[2048,512]{1,0:T(8,128)}, f32[2048,512]{1,0:T(8,128)}), (f32[2048,512]{1,0:T(8,128)}, f32[2048,512]{1,0:T(8,128)})) %all-reduce.3.cloned.1.call-update) | async-done | bytes 8388624 | tf_op jit(solution)/shard_map/psum | solution.py:115
  837.6 7.7 multiply_convert_fusion.1
  845.3 163.6 %while.27 = (s32[]{:T(128)}, f32[2048,512]{1,0:T(8,128)}, f32[3,2048]{1,0:T(4,128)}, f32[3,2048]{1,0:T(4,128)S(1)}, bf16[2048,512]{1,0:T(8,128)(2,1)}, /*index=5...) while((s32[]{:T(128)}, f32[2048,512]{1,0:T(8,128)}, ...), condition=%wide.region_8.9_spmd.clone, body=%wide.region_7.8_spmd.clone.sunk | while | flops 2163212288 | bytes 17948888 | solution.py:135
  860.8 0.9 constant_dynamic-slice_fusion.8
  861.7 17.6 %fusion.88 = f32[2048,512]{1,0:T(8,128)} fusion(f32[2048]{0:T(1024)S(1)} %bitcast.113, f32[512]{0:T(512)S(1)} %bitcast.131, f32[2048]{0:T(1024)S(1)} %bitcast.115, f32[512]{0:T(512)S(1)} %bitcast.129, f32[2048]{0:T(1024)S(1)} %bitcast.111, f32[512]{0:T(512)S(1)} %bitcast.127, bf16[2048,512]{1,0:T(8,128)(2,1)} %get-tuple-element.371, s32[]{:T(128)S(6)} %select_n.66), kind=kOutput, calls=%fused_computation.31.clone.1 | convolution fusion | flops 1080033280 | bytes 4749316 | tf_op jit(solution)/shard_map/while/body/eval_jaxpr/dot_general | solution.py:128
  879.3 18.0 %fusion.89 = f32[2048,512]{1,0:T(8,128)} fusion(f32[2048,512]{1,0:T(8,128)} %fusion.88, f32[2048,512]{1,0:T(8,128)} %get-tuple-element.356, f32[2048]{0:T(1024)S(1)} %bitcast.114, f32[512]{0:T(512)S(1)} %bitcast.132, f32[2048]{0:T(1024)S(1)} %bitcast.116, f32[512]{0:T(512)S(1)} %bitcast.130, f32[2048]{0:T(1024)S(1)} %bitcast.112, ...), kind=kOutput, calls=%fused_computation.27.clone.1 | convolution fusion | flops 1083179008 | bytes 13137925 | tf_op jit(solution)/shard_map/while/body/eval_jaxpr/dot_general | solution.py:131
  897.3 0.9 constant_dynamic-slice_fusion.8
  898.2 17.6 %fusion.88 = f32[2048,512]{1,0:T(8,128)} fusion(f32[2048]{0:T(1024)S(1)} %bitcast.113, f32[512]{0:T(512)S(1)} %bitcast.131, f32[2048]{0:T(1024)S(1)} %bitcast.115, f32[512]{0:T(512)S(1)} %bitcast.129, f32[2048]{0:T(1024)S(1)} %bitcast.111, f32[512]{0:T(512)S(1)} %bitcast.127, bf16[2048,512]{1,0:T(8,128)(2,1)} %get-tuple-element.371, s32[]{:T(128)S(6)} %select_n.66), kind=kOutput, calls=%fused_computation.31.clone.1 | convolution fusion | flops 1080033280 | bytes 4749316 | tf_op jit(solution)/shard_map/while/body/eval_jaxpr/dot_general | solution.py:128
  915.8 18.6 %fusion.89 = f32[2048,512]{1,0:T(8,128)} fusion(f32[2048,512]{1,0:T(8,128)} %fusion.88, f32[2048,512]{1,0:T(8,128)} %get-tuple-element.356, f32[2048]{0:T(1024)S(1)} %bitcast.114, f32[512]{0:T(512)S(1)} %bitcast.132, f32[2048]{0:T(1024)S(1)} %bitcast.116, f32[512]{0:T(512)S(1)} %bitcast.130, f32[2048]{0:T(1024)S(1)} %bitcast.112, ...), kind=kOutput, calls=%fused_computation.27.clone.1 | convolution fusion | flops 1083179008 | bytes 13137925 | tf_op jit(solution)/shard_map/while/body/eval_jaxpr/dot_general | solution.py:131
  934.5 0.9 constant_dynamic-slice_fusion.8
  935.4 17.6 %fusion.88 = f32[2048,512]{1,0:T(8,128)} fusion(f32[2048]{0:T(1024)S(1)} %bitcast.113, f32[512]{0:T(512)S(1)} %bitcast.131, f32[2048]{0:T(1024)S(1)} %bitcast.115, f32[512]{0:T(512)S(1)} %bitcast.129, f32[2048]{0:T(1024)S(1)} %bitcast.111, f32[512]{0:T(512)S(1)} %bitcast.127, bf16[2048,512]{1,0:T(8,128)(2,1)} %get-tuple-element.371, s32[]{:T(128)S(6)} %select_n.66), kind=kOutput, calls=%fused_computation.31.clone.1 | convolution fusion | flops 1080033280 | bytes 4749316 | tf_op jit(solution)/shard_map/while/body/eval_jaxpr/dot_general | solution.py:128
  953.0 18.6 %fusion.89 = f32[2048,512]{1,0:T(8,128)} fusion(f32[2048,512]{1,0:T(8,128)} %fusion.88, f32[2048,512]{1,0:T(8,128)} %get-tuple-element.356, f32[2048]{0:T(1024)S(1)} %bitcast.114, f32[512]{0:T(512)S(1)} %bitcast.132, f32[2048]{0:T(1024)S(1)} %bitcast.116, f32[512]{0:T(512)S(1)} %bitcast.130, f32[2048]{0:T(1024)S(1)} %bitcast.112, ...), kind=kOutput, calls=%fused_computation.27.clone.1 | convolution fusion | flops 1083179008 | bytes 13137925 | tf_op jit(solution)/shard_map/while/body/eval_jaxpr/dot_general | solution.py:131
  971.6 0.9 constant_dynamic-slice_fusion.8
  972.5 17.6 %fusion.88 = f32[2048,512]{1,0:T(8,128)} fusion(f32[2048]{0:T(1024)S(1)} %bitcast.113, f32[512]{0:T(512)S(1)} %bitcast.131, f32[2048]{0:T(1024)S(1)} %bitcast.115, f32[512]{0:T(512)S(1)} %bitcast.129, f32[2048]{0:T(1024)S(1)} %bitcast.111, f32[512]{0:T(512)S(1)} %bitcast.127, bf16[2048,512]{1,0:T(8,128)(2,1)} %get-tuple-element.371, s32[]{:T(128)S(6)} %select_n.66), kind=kOutput, calls=%fused_computation.31.clone.1 | convolution fusion | flops 1080033280 | bytes 4749316 | tf_op jit(solution)/shard_map/while/body/eval_jaxpr/dot_general | solution.py:128
  990.1 18.6 %fusion.89 = f32[2048,512]{1,0:T(8,128)} fusion(f32[2048,512]{1,0:T(8,128)} %fusion.88, f32[2048,512]{1,0:T(8,128)} %get-tuple-element.356, f32[2048]{0:T(1024)S(1)} %bitcast.114, f32[512]{0:T(512)S(1)} %bitcast.132, f32[2048]{0:T(1024)S(1)} %bitcast.116, f32[512]{0:T(512)S(1)} %bitcast.130, f32[2048]{0:T(1024)S(1)} %bitcast.112, ...), kind=kOutput, calls=%fused_computation.27.clone.1 | convolution fusion | flops 1083179008 | bytes 13137925 | tf_op jit(solution)/shard_map/while/body/eval_jaxpr/dot_general | solution.py:131
  1009.0 3.9 convert_element_type.67
  1012.9 0.0 reduce-scatter.3.cloned.1.call-update
  1012.9 0.0 all-gather.5.cloned.1.call-start
  1013.0 0.9 collective-permute-start.2
  1013.9 0.4 broadcast_select_fusion.1
  1014.3 1.8 collective-permute-start
  1016.2 5.8 collective-permute-start.1
  1022.0 0.1 copy.18
  1022.0 0.1 reshape.112
  1022.2 0.6 gather_fusion.1
  1022.9 1.4 broadcast_subtract_fusion
  1024.4 2.8 fusion.46
  1027.2 0.2 pad_maximum_fusion
  1027.3 2.5 gather_fusion
  1029.8 8.2 fusion.36
  1038.1 1.9 copy.22
  1040.0 9.6 reduce-scatter.3.cloned.1.call-done
  1049.6 3.0 fusion.58
  1052.6 0.0 all-gather.5.cloned.1.call-update
  1052.6 0.0 reduce-scatter.5.cloned.1.call-start
  1052.7 36.2 %all-gather.5.cloned.1.call-done = bf16[2048,512]{1,0:T(8,128)(2,1)} async-done(((bf16[2048,256]{1,0:T(8,128)(2,1)}), bf16[2048,512]{1,0:T(8,128)(2,1)}) %all-gather.5.cloned.1.call-update) | async-done | bytes 2097168 | tf_op jit(solution)/shard_map/all_gather | solution.py:147
  1088.9 2.1 fusion.40
  1091.0 5.8 convolution_convert_fusion
  1096.8 0.0 reduce-scatter.5.cloned.1.call-update
  1096.8 35.5 %reduce-scatter.5.cloned.1.call-done = bf16[2048,256]{1,0:T(8,128)(2,1)} async-done(((bf16[2048,512]{1,0:T(8,128)(2,1)}), bf16[2048,256]{1,0:T(8,128)(2,1)}) %reduce-scatter.5.cloned.1.call-update) | async-done | bytes 1048592 | tf_op jit(solution)/shard_map/reduce_scatter | solution.py:157
  1132.2 3.4 add_convert_fusion
  (45 shorter events, 0.3 us)
Async XLA Ops:
  6.5 1084.4 %copy-start = (bf16[512,512]{1,0:T(8,128)(2,1)S(1)}, bf16[512,512]{1,0:T(8,128)(2,1)}, u32[]{:S(2)}) copy-start(bf16[512,512]{1,0:T(8,128)(2,1)} %param.25) | copy-start | bytes 1572868
  6.5 43.1 %copy-start.2 = (f32[3,2048]{1,0:T(4,128)S(1)}, f32[3,2048]{1,0:T(4,128)}, u32[]{:S(2)}) copy-start(f32[3,2048]{1,0:T(4,128)} %param.16) | copy-start | bytes 73732
  6.5 41.3 %all-gather.3.cloned.1.call-start = ((), (), s32[]{:S(2)}) async-start(), calls=%async_computation.2 | async-start | bytes 3145728 | tf_op jit(solution)/shard_map/all_gather | solution.py:95
  7.3 830.3 %all-reduce.3.cloned.1.call-start = ((), (), s32[]{:S(2)}) async-start(), calls=%async_computation.6 | async-start | bytes 16777216 | tf_op jit(solution)/shard_map/psum | solution.py:115
  175.1 0.7 copy-start.5
  175.1 874.5 %reduce-scatter.3.cloned.1.call-start = ((), (), s32[]{:S(2)}) async-start(), calls=%async_computation.3 | async-start | bytes 3145728 | tf_op jit(solution)/shard_map/reduce_scatter | solution.py:143
  1008.9 4.9 copy-start.1
  1009.0 13.0 %copy-start.4 = (s32[16,3]{0,1:T(4,128)S(1)}, s32[16,3]{0,1:T(4,128)}, u32[]{:S(2)}) copy-start(s32[16,3]{0,1:T(4,128)} %param.18) | copy-start | bytes 580
  1009.0 13.2 %copy-start.3 = (f32[4,512]{1,0:T(4,128)S(1)}, f32[4,512]{1,0:T(4,128)}, u32[]{:S(2)}) copy-start(f32[4,512]{1,0:T(4,128)} %param.22) | copy-start | bytes 24580
  1009.0 13.2 %copy-start.8 = (f32[4]{0:T(128)S(1)}, f32[4]{0:T(128)}, u32[]{:S(2)}) copy-start(f32[4]{0:T(128)} %param.21) | copy-start | bytes 52
  1012.9 76.0 %all-gather.5.cloned.1.call-start = ((), (), s32[]{:S(2)}) async-start(), calls=%async_computation.4 | async-start | bytes 3145728 | tf_op jit(solution)/shard_map/all_gather | solution.py:147
  1013.0 9.2 collective-permute-start.2
  1013.9 8.3 collective-permute-start.3
  1014.3 12.8 %collective-permute-start = (bf16[2,128,256]{2,1,0:T(8,128)(2,1)S(1)}, bf16[2,128,256]{2,1,0:T(8,128)(2,1)S(1)}, u32[]{:S(2)}, u32[]{:S(2)}) collective-permute-start(bf16[2,128,256]{2,1,0:T(8,128)(2,1)S(1)} %bitcast.124), channel_id=1, source_target_pairs={{0,2},{2,4},{4,6},{6,8},{8,10},{10,12},{12,14},{14,16},{16,18},{18... | collective-permute-start | bytes 393224 | tf_op jit(solution)/shard_map/ppermute | solution.py:22
  1016.2 11.0 collective-permute-start.1
  1040.0 51.0 %copy-start.6 = (bf16[512,512]{1,0:T(8,128)(2,1)S(1)}, bf16[512,512]{1,0:T(8,128)(2,1)}, u32[]{:S(2)}) copy-start(bf16[512,512]{1,0:T(8,128)(2,1)} %param.24) | copy-start | bytes 1572868
  1040.0 51.0 %copy-start.7 = (f32[512]{0:T(512)S(1)}, f32[512]{0:T(512)}, u32[]{:S(2)}) copy-start(f32[512]{0:T(512)} %param.23) | copy-start | bytes 6148
  1052.6 79.6 %reduce-scatter.5.cloned.1.call-start = ((), (), s32[]{:S(2)}) async-start(), calls=%async_computation.5 | async-start | bytes 3145728 | tf_op jit(solution)/shard_map/reduce_scatter | solution.py:157
Sparse Core Ops, SparseCore 0:
  9.0 38.7 all-gather.2
  175.2 662.3 all-reduce.2
  1013.0 36.5 reduce-scatter.2
  1052.7 36.1 all-gather.4
  1096.9 35.3 reduce-scatter.4
where the time goes:
time: 1160 us; the launch traced here: 1140 us
  waiting for transfers between devices  619 us (53%)
  matrix products  280 us (24%)
  blocking collectives  163 us (14%)
  other arithmetic  28.1 us (2%)
  loops' own time  15.7 us (1%)
  between operations  15.1 us (1%)
  local copies, waits for them, and re-layouts  12.9 us (1%)
    psum x1, waiting for transfers between devices, shards(): cos_total, sin_total = lax.psum((cos_sum, sin_sum), 'cells')  497 us
    psum x1, blocking collectives, shards(): count = lax.psum(jnp.sum(occupancy).astype(jnp.float32), 'cells')  163 us
    dot_general x4, matrix products, add_block(): lax.dot_general(sine_block, sin_part, contract, preferred_element_type=jn...  73.9 us
    dot_general x4, matrix products, add_block(): lax.dot_general(cosine_block, cos_part, contract, preferred_element_type=...  70.4 us
    dot_general x4, matrix products, forward(): jnp.dot(sine_block, masked_whole, preferred_element_type=jnp.float32)  61.4 us
    dot_general x4, matrix products, forward(): jnp.dot(cosine_block, masked_whole, preferred_element_type=jnp.float32)  60.7 us
    all_gather x1, waiting for transfers between devices, shards(): whole = lax.all_gather(features, 'waves', axis=1, tiled=True)  39.8 us
    all_gather x1, waiting for transfers between devices, shards(): lax.all_gather(merged_part.astype(jnp.bfloat16), 'waves', axis=1, tiled=T...  36.2 us
  transfers between devices with their start and end apart: 9, of which 5 were waited for; matrix products, arithmetic and copies ran while one was open for 2% of the time, Pallas kernels for 0%

commit v1 on v0

v1 whole, which is shorter than its diff:
```python
import functools
import math

import jax
import jax.numpy as jnp
from jax import lax
from jax.experimental import pallas as pl
from jax.experimental.pallas import tpu as pltpu
from jax.sharding import PartitionSpec as P

F = 512
K = 4096
CAP = 128
HW = 2
NB = 3
G = 4
EPS = 1e-06
WAVES = 2
PART = 256
ROWS = 2048
LOCAL = 16
LENGTH = 1024.0
KP = 128
TILE = 256
CHUNK = 128
HALF = ROWS // 2
BF = jnp.bfloat16
F32 = jnp.float32
MESH = pl.DeviceIdType.MESH
TURN = 1.0 / (2.0 * math.pi)
LOG2E = 1.4426950408889634

SIN = (4.442867900911655, -7.307443330487869, 3.594787161239145, -0.784371485095076)
COS = (1.4142040799995839, -6.977641979004694, 5.715237169770743, -1.7283443233022544)


def params(**more):
    return pltpu.CompilerParams(vmem_limit_bytes=62 << 20, **more)


def split3(v):
    a = v.astype(BF).astype(F32)
    b = (v - a).astype(BF).astype(F32)
    c = ((v - a) - b).astype(BF).astype(F32)
    return a, b, c


def prologue(pos_ref, wave_ref, left_ref, right_ref, lrows, rrows):
    first = lax.axis_index("cells") * LOCAL
    lrows[...] = jnp.zeros_like(lrows)
    rrows[...] = jnp.zeros_like(rrows)
    cell = lax.broadcasted_iota(jnp.int32, (1, ROWS), 1) // CAP
    for part in range(3):
        v = pos_ref[part : part + 1, :]
        if part == 0:
            v = v - (cell + first).astype(F32)
        a, b, _ = split3(v)
        k1, k2, _ = split3(wave_ref[part : part + 1, :] * TURN)
        for n, (l, r) in enumerate(((a, k1), (a, k2), (b, k1), (b, k2))):
            row = part * 4 + n
            lrows[row : row + 1, :] = l
            rrows[row : row + 1, :] = r
    along = wave_ref[0:1, :] * TURN
    for c in range(LOCAL):
        whole = along * (first + c).astype(F32)
        whole = whole - lax.round(whole, lax.RoundingMethod.TO_NEAREST_EVEN)
        for n, piece in enumerate(split3(whole)):
            row = 12 + 3 * c + n
            lrows[row : row + 1, :] = (cell == c).astype(F32)
            rrows[row : row + 1, :] = piece
    left_ref[...] = lrows[...].T.astype(BF)
    right_ref[...] = rrows[...].astype(BF)


def phase_operands(positions, waves):
    return pl.pallas_call(
        prologue,
        out_shape=(
            jax.ShapeDtypeStruct((ROWS, KP), BF),
            jax.ShapeDtypeStruct((KP, K), BF),
        ),
        scratch_shapes=[pltpu.VMEM((KP, ROWS), F32), pltpu.VMEM((KP, K), F32)],
        compiler_params=params(),
    )(positions, waves)


def trig(turns):
    r = turns - lax.round(turns, lax.RoundingMethod.TO_NEAREST_EVEN)
    s = r * r
    half_sin = r * (SIN[0] + s * (SIN[1] + s * (SIN[2] + s * SIN[3])))
    half_cos = COS[0] + s * (COS[1] + s * (COS[2] + s * COS[3]))
    return (1.0 - half_sin * half_sin).astype(BF), (half_sin * half_cos).astype(BF)


def forward_kernel(left_ref, right_ref, feats_ref, cos_ref, sin_ref, sum_ref):
    cos_sum = jnp.zeros((PART, TILE), F32)
    sin_sum = jnp.zeros((PART, TILE), F32)
    for b in range(ROWS // TILE):
        rows = slice(b * TILE, (b + 1) * TILE)
        turns = jnp.dot(left_ref[rows, :], right_ref[...], preferred_element_type=F32)
        cosine, sine = trig(turns)
        cos_ref[rows, :] = cosine
        sin_ref[rows, :] = sine
        block = feats_ref[:, rows]
        cos_sum += jnp.dot(block, cosine, preferred_element_type=F32)
        sin_sum += jnp.dot(block, sine, preferred_element_type=F32)
    for n in range(TILE // CHUNK):
        lanes = slice(n * CHUNK, (n + 1) * CHUNK)
        sum_ref[0, n] = cos_sum[:, lanes].astype(BF)
        sum_ref[1, n] = sin_sum[:, lanes].astype(BF)


def forward(left, right, feats):
    return pl.pallas_call(
        forward_kernel,
        grid=(K // TILE,),
        in_specs=[
            pl.BlockSpec((ROWS, KP), lambda j: (0, 0)),
            pl.BlockSpec((KP, TILE), lambda j: (0, j)),
            pl.BlockSpec((PART, ROWS), lambda j: (0, 0)),
        ],
        out_specs=[
            pl.BlockSpec((ROWS, TILE), lambda j: (0, j)),
            pl.BlockSpec((ROWS, TILE), lambda j: (0, j)),
            pl.BlockSpec((2, TILE // CHUNK, PART, CHUNK), lambda j: (0, j, 0, 0)),
        ],
        out_shape=(
            jax.ShapeDtypeStruct((ROWS, K), BF),
            jax.ShapeDtypeStruct((ROWS, K), BF),
            jax.ShapeDtypeStruct((2, K // CHUNK, PART, CHUNK), BF),
        ),
        compiler_params=params(),
    )(left, right, feats)


def place():
    cells = lax.axis_index("cells")
    return cells // 16, (cells // 8) % 2, (cells // 2) % 4, cells % 2


def cell_index(z, x, y, core):
    return ((z * 2 + x) * 4 + y) * 2 + core


def exchange_kernel(
    sum_ref, filt_ref, feats_ref, pos_ref, count_ref, in_ref, out_ref,
    all_ref, in2_ref, out2_ref, edge_ref, edgepos_ref,
    r1, s1, r2a, r2b, s2a, s2b, r3a, r3b, s3a, s3b, r4a, r4b,
    mine, theirs, counts, rcounts, send_sem, recv_sem, local_sem,
):
    z, x, y, core = place()
    waves = lax.axis_index("waves")
    cells = lax.axis_index("cells")
    other = 1 - waves

    def at(cell):
        return {"cells": cell, "waves": waves}

    def sibling():
        return at(cell_index(z, x, y, 1 - core))

    def along_y(d):
        return at(cell_index(z, x, lax.rem(y + d, 4), core))

    def along_z(d):
        return at(cell_index(lax.rem(z + d, 4), x, y, core))

    def along_x():
        return at(cell_index(z, 1 - x, y, core))

    above = at(lax.rem(cells + 1, 64))
    below = at(lax.rem(cells + 63, 64))
    partner = {"cells": cells, "waves": other}
    peers = [sibling(), along_x(), partner, above, below]
    peers += [along_y(d) for d in (1, 2, 3)] + [along_z(d) for d in (1, 2, 3)]
    barrier = pltpu.get_barrier_semaphore()
    for peer in peers:
        pl.semaphore_signal(barrier, inc=1, device_id=peer, device_id_type=MESH)
    pl.semaphore_wait(barrier, len(peers))

    taken = [0]

    def remote(src, dst, device):
        n = taken[0]
        taken[0] += 1
        copy = pltpu.make_async_remote_copy(
            src_ref=src, dst_ref=dst, send_sem=send_sem.at[n], recv_sem=recv_sem.at[n],
            device_id=device, device_id_type=MESH,
        )
        copy.start()
        return copy

    one = [
        remote(sum_ref.at[1 - core], r1, sibling()),
        remote(count_ref, rcounts.at[0], sibling()),
    ]
    block = y * 8 + z * 2 + x
    row = pl.multiple_of(lax.rem(block, 16) * CHUNK, CHUNK)
    column = pl.multiple_of(other * PART, PART)
    own_column = pl.multiple_of(waves * PART, PART)
    early = [
        remote(filt_ref.at[pl.ds(row, CHUNK), pl.ds(column, PART)], theirs, partner),
        remote(feats_ref.at[pl.ds(0, 2 * CAP)], edge_ref.at[1], below),
        remote(feats_ref.at[pl.ds(ROWS - 2 * CAP, 2 * CAP)], edge_ref.at[0], above),
        remote(pos_ref.at[:, pl.ds(0, 2 * CAP)], edgepos_ref.at[1], below),
        remote(pos_ref.at[:, pl.ds(ROWS - 2 * CAP, 2 * CAP)], edgepos_ref.at[0], above),
        remote(in_ref, in2_ref, partner),
        remote(out_ref, out2_ref, partner),
    ]
    local = pltpu.make_async_copy(
        filt_ref.at[pl.ds(row, CHUNK), pl.ds(own_column, PART)], mine, local_sem
    )
    local.start()

    for copy in one:
        copy.wait()

    def add1(n, carry):
        yy, zz, xx = n // 8, (n // 2) % 4, n % 2
        s1[yy, zz, xx] = (
            sum_ref[core, yy, zz, xx].astype(F32) + r1[yy, zz, xx].astype(F32)
        ).astype(BF)
        return carry

    lax.fori_loop(0, 32, add1, 0)
    counts[0] = count_ref[...] + rcounts[0]

    two = []
    for d in (1, 2, 3):
        ty, tz = lax.rem(y + d, 4), lax.rem(z + d, 4)
        two += [
            remote(s1.at[ty, :, :, pl.ds(0, CHUNK), :], r2a.at[d - 1], along_y(d)),
            remote(s1.at[:, tz, :, pl.ds(CHUNK, CHUNK), :], r2b.at[d - 1], along_z(d)),
            remote(counts.at[0], rcounts.at[d], along_y(d)),
        ]
    for copy in two:
        copy.wait()

    def add2(n, carry):
        p, xx = n // 2, n % 2
        a = s1[y, p, xx, 0:CHUNK, :].astype(F32)
        b = s1[p, z, xx, CHUNK:PART, :].astype(F32)
        for d in range(3):
            a += r2a[d, p, xx].astype(F32)
            b += r2b[d, p, xx].astype(F32)
        s2a[p, xx] = a.astype(BF)
        s2b[p, xx] = b.astype(BF)
        return carry

    lax.fori_loop(0, 8, add2, 0)
    counts[1] = counts[0] + rcounts[1] + rcounts[2] + rcounts[3]

    three = []
    for d in (1, 2, 3):
        ty, tz = lax.rem(y + d, 4), lax.rem(z + d, 4)
        three += [
            remote(s2a.at[tz], r3a.at[d - 1], along_z(d)),
            remote(s2b.at[ty], r3b.at[d - 1], along_y(d)),
            remote(counts.at[1], rcounts.at[3 + d], along_z(d)),
        ]
    for copy in three:
        copy.wait()
    for xx in range(2):
        a, b = s2a[z, xx].astype(F32), s2b[y, xx].astype(F32)
        for d in range(3):
            a += r3a[d, xx].astype(F32)
            b += r3b[d, xx].astype(F32)
        s3a[xx] = a.astype(BF)
        s3b[xx] = b.astype(BF)
    counts[2] = counts[1] + rcounts[4] + rcounts[5] + rcounts[6]

    four = [
        remote(s3a.at[1 - x], r4a, along_x()),
        remote(s3b.at[1 - x], r4b, along_x()),
        remote(counts.at[2], rcounts.at[7], along_x()),
    ]
    for copy in four:
        copy.wait()
    total_a = s3a[x].astype(F32) + r4a[...].astype(F32)
    total_b = s3b[x].astype(F32) + r4b[...].astype(F32)
    root = jnp.sqrt((counts[2] + rcounts[7])[0:1, 0:1])
    local.wait()
    early[0].wait()
    here = (block // 16) == waves
    filters = jnp.where(here, mine[...], theirs[...])
    all_ref[core, y, z, x, :, 0:CHUNK] = (
        filters[:, 0:CHUNK] * (total_a.T / root)
    ).astype(BF)
    all_ref[core, y, z, x, :, CHUNK:PART] = (
        filters[:, CHUNK:PART] * (total_b.T / root)
    ).astype(BF)

    own = all_ref.at[core, y, z, x]
    remote(own, own, along_x()).wait()
    steps = []
    lane_a, lane_b = pl.ds(0, CHUNK), pl.ds(CHUNK, CHUNK)
    for d in (1, 2, 3):
        piece = all_ref.at[core, y, z, :, :, lane_a]
        steps.append(remote(piece, piece, along_z(d)))
        piece = all_ref.at[core, y, z, :, :, lane_b]
        steps.append(remote(piece, piece, along_y(d)))
    for copy in steps:
        copy.wait()
    steps = []
    for d in (1, 2, 3):
        piece = all_ref.at[core, y, :, :, :, lane_a]
        steps.append(remote(piece, piece, along_y(d)))
        piece = all_ref.at[core, :, z, :, :, lane_b]
        steps.append(remote(piece, piece, along_z(d)))
    for copy in steps:
        copy.wait()
    piece = all_ref.at[core]
    remote(piece, piece, sibling()).wait()
    for copy in early[1:]:
        copy.wait()


def exchange(sums, filters, feats, pos8, count, in_weight, out_weight):
    vmem = pl.BlockSpec(memory_space=pltpu.VMEM)
    hbm = pl.BlockSpec(memory_space=pl.ANY)
    return pl.pallas_call(
        exchange_kernel,
        in_specs=[vmem, hbm, hbm, hbm, vmem, hbm, hbm],
        out_specs=[vmem, hbm, hbm, hbm, hbm],
        out_shape=(
            jax.ShapeDtypeStruct((2, 4, 4, 2, CHUNK, PART), BF),
            jax.ShapeDtypeStruct(in_weight.shape, BF),
            jax.ShapeDtypeStruct(out_weight.shape, BF),
            jax.ShapeDtypeStruct((2, 2 * CAP, PART), BF),
            jax.ShapeDtypeStruct((2, 8, 2 * CAP), F32),
        ),
        scratch_shapes=[
            pltpu.VMEM((4, 4, 2, PART, CHUNK), BF),
            pltpu.VMEM((4, 4, 2, PART, CHUNK), BF),
            pltpu.VMEM((3, 4, 2, CHUNK, CHUNK), BF),
            pltpu.VMEM((3, 4, 2, CHUNK, CHUNK), BF),
            pltpu.VMEM((4, 2, CHUNK, CHUNK), BF),
            pltpu.VMEM((4, 2, CHUNK, CHUNK), BF),
            pltpu.VMEM((3, 2, CHUNK, CHUNK), BF),
            pltpu.VMEM((3, 2, CHUNK, CHUNK), BF),
            pltpu.VMEM((2, CHUNK, CHUNK), BF),
            pltpu.VMEM((2, CHUNK, CHUNK), BF),
            pltpu.VMEM((CHUNK, CHUNK), BF),
            pltpu.VMEM((CHUNK, CHUNK), BF),
            pltpu.VMEM((CHUNK, PART), F32),
            pltpu.VMEM((CHUNK, PART), F32),
            pltpu.VMEM((3, 8, 128), F32),
            pltpu.VMEM((8, 8, 128), F32),
            pltpu.SemaphoreType.DMA((48,)),
            pltpu.SemaphoreType.DMA((48,)),
            pltpu.SemaphoreType.DMA,
        ],
        compiler_params=params(collective_id=0, has_side_effects=True),
    )(sums, filters, feats, pos8, count, in_weight, out_weight)


def merge_kernel(
    neigh_ref, fall_ref, cos_ref, sin_ref, all_ref, feats_ref, wide_ref, widepos_ref,
    column_ref, mix_ref, merged_ref,
):
    far = jnp.dot(cos_ref[...], all_ref[0:K, :], preferred_element_type=F32)
    far += jnp.dot(sin_ref[...], all_ref[K:, :], preferred_element_type=F32)
    base = feats_ref[...].astype(F32) + far * (1.0 / math.sqrt(K))
    step = pl.program_id(0)
    for c in range(TILE // CAP):
        cell = step * (TILE // CAP) + c
        rows = slice(c * CAP, (c + 1) * CAP)
        here = [column_ref[rows, p : p + 1] for p in range(3)]
        sums = [jnp.zeros((CAP, PART), F32) for _ in range(G)]
        for n in range(NB):
            partner = cell + HW + neigh_ref[cell * NB + n]
            lanes = pl.ds(pl.multiple_of(partner * CAP, CAP), CAP)
            there = widepos_ref[:, lanes]
            feats = wide_ref[lanes, :]
            squared = jnp.zeros((CAP, CAP), F32)
            for p in range(3):
                d = here[p] - there[p : p + 1, :]
                squared += d * d
            for g in range(G):
                weight = jnp.exp(-fall_ref[g] * squared).astype(BF)
                sums[g] += jnp.dot(weight, feats, preferred_element_type=F32)
        near = jnp.zeros((CAP, PART), F32)
        for g in range(G):
            near += sums[g] * mix_ref[g : g + 1, :]
        merged_ref[rows, :] = base[rows, :] + near


def merge(neigh, fall, cosine, sine, filtered, feats, wide, widepos, column, mix):
    once = pl.Buffered(1)
    return pl.pallas_call(
        merge_kernel,
        grid=(ROWS // TILE,),
        in_specs=[
            pl.BlockSpec(memory_space=pltpu.SMEM),
            pl.BlockSpec(memory_space=pltpu.SMEM),
            pl.BlockSpec((TILE, K), lambda i: (i, 0)),
            pl.BlockSpec((TILE, K), lambda i: (i, 0)),
            pl.BlockSpec((2 * K, PART), lambda i: (0, 0), pipeline_mode=once),
            pl.BlockSpec((TILE, PART), lambda i: (i, 0)),
            pl.BlockSpec((ROWS + 4 * CAP, PART), lambda i: (0, 0)),
            pl.BlockSpec((8, ROWS + 4 * CAP), lambda i: (0, 0)),
            pl.BlockSpec((TILE, 3), lambda i: (i, 0)),
            pl.BlockSpec((G, PART), lambda i: (0, 0)),
        ],
        out_specs=pl.BlockSpec((TILE, PART), lambda i: (i, 0)),
        out_shape=jax.ShapeDtypeStruct((ROWS, PART), F32),
        compiler_params=params(),
    )(neigh, fall, cosine, sine, filtered, feats, wide, widepos, column, mix)


PIECES = 4
PIECE = HALF // PIECES


def mlp_kernel(
    merged_ref, gain_ref, in_ref, in2_ref, out_ref, out2_ref, result_ref,
    outgoing, incoming, back, returned, send_sem, recv_sem,
):
    waves = lax.axis_index("waves")
    other = 1 - waves
    partner = {"cells": lax.axis_index("cells"), "waves": other}
    barrier = pltpu.get_barrier_semaphore()
    pl.semaphore_signal(barrier, inc=1, device_id=partner, device_id_type=MESH)
    pl.semaphore_wait(barrier, 1)

    def remote(src, dst, n):
        copy = pltpu.make_async_remote_copy(
            src_ref=src, dst_ref=dst, send_sem=send_sem.at[n], recv_sem=recv_sem.at[n],
            device_id=partner, device_id_type=MESH,
        )
        copy.start()
        return copy

    own = pl.multiple_of(waves * PART, PART)
    far = pl.multiple_of(other * PART, PART)
    there = []
    for q in range(PIECES):
        rows = pl.ds(pl.multiple_of(other * HALF + q * PIECE, PIECE), PIECE)
        outgoing[q] = merged_ref[rows, :].astype(BF)
        there.append(remote(outgoing.at[q], incoming.at[q], q))
    returns = []
    for q in range(PIECES):
        there[q].wait()
        rows = pl.ds(pl.multiple_of(waves * HALF + q * PIECE, PIECE), PIECE)
        mine = merged_ref[rows, :]
        theirs = incoming[q].astype(F32)
        square = jnp.sum(mine * mine + theirs * theirs, axis=1, keepdims=True)
        scale = lax.rsqrt(square * (1.0 / F) + EPS)
        mine_n = (mine * scale * gain_ref[:, pl.ds(own, PART)]).astype(BF)
        theirs_n = (theirs * scale * gain_ref[:, pl.ds(far, PART)]).astype(BF)
        add_mine, add_theirs = mine, jnp.zeros_like(mine)
        for first, second in ((in_ref, out_ref), (in2_ref, out2_ref)):
            hidden = jnp.dot(
                mine_n, first[pl.ds(own, PART), :], preferred_element_type=F32
            ) + jnp.dot(theirs_n, first[pl.ds(far, PART), :], preferred_element_type=F32)
            hidden = (hidden / (1.0 + jnp.exp(-hidden))).astype(BF)
            add_mine += jnp.dot(
                hidden, second[:, pl.ds(own, PART)], preferred_element_type=F32
            )
            add_theirs += jnp.dot(
                hidden, second[:, pl.ds(far, PART)], preferred_element_type=F32
            )
        back[q] = add_theirs.astype(BF)
        returns.append(remote(back.at[q], returned.at[q], PIECES + q))
        result_ref[rows, :] = add_mine.astype(BF)
    for q in range(PIECES):
        returns[q].wait()
        rows = pl.ds(pl.multiple_of(other * HALF + q * PIECE, PIECE), PIECE)
        result_ref[rows, :] = (merged_ref[rows, :] + returned[q].astype(F32)).astype(BF)


def mlp(merged, gain, in_weight, in2, out_weight, out2):
    vmem = pl.BlockSpec(memory_space=pltpu.VMEM)
    return pl.pallas_call(
        mlp_kernel,
        in_specs=[vmem] * 6,
        out_specs=vmem,
        out_shape=jax.ShapeDtypeStruct((ROWS, PART), BF),
        scratch_shapes=[pltpu.VMEM((PIECES, PIECE, PART), BF)] * 4
        + [pltpu.SemaphoreType.DMA((2 * PIECES,))] * 2,
        compiler_params=params(collective_id=1, has_side_effects=True),
    )(merged, gain, in_weight, in2, out_weight, out2)


def shards(
    features, positions, occupancy, neighbours, wavevectors, filters,
    falloffs, mixing, norm_gain, in_weight, out_weight,
):
    cells = lax.axis_index("cells")
    waves = lax.axis_index("waves")
    is_live = (
        jnp.arange(CAP, dtype=jnp.int32)[None, :] < occupancy[:, None]
    ).reshape(ROWS, 1)
    masked = jnp.where(is_live, features, jnp.zeros_like(features))
    whole_waves = lax.all_gather(wavevectors, "waves", axis=1, tiled=True)
    left, right = phase_operands(positions, whole_waves)
    cosine, sine, sums = forward(left, right, masked.T)
    pos8 = jnp.pad(positions, ((0, 5), (0, 0)))
    count = jnp.full((8, 128), jnp.sum(occupancy).astype(F32))
    filtered, in2, out2, edges, edge_pos = exchange(
        sums.reshape(2, 4, 4, 2, PART, CHUNK), filters, masked, pos8, count,
        in_weight, out_weight,
    )
    length = jnp.float32(LENGTH)
    shift_low = jnp.where(cells == 0, -length, 0.0)
    shift_high = jnp.where(cells == 63, length, 0.0)
    first = jnp.zeros((8, 1), F32).at[0].set(1.0)
    widepos = jnp.concatenate(
        [edge_pos[0] + first * shift_low, pos8, edge_pos[1] + first * shift_high], axis=1
    )
    wide = jnp.concatenate([edges[0], masked, edges[1]], axis=0)
    mix = lax.dynamic_slice_in_dim(mixing, waves * PART, PART, 1)
    merged = merge(
        neighbours.reshape(LOCAL * NB), falloffs, cosine, sine,
        filtered.reshape(2 * K, PART), features, wide, widepos, positions.T, mix,
    )
    return mlp(merged, norm_gain[None, :], in_weight, in2, out_weight, out2)


def solution(mesh):
    placed = (
        P("cells", "waves"),
        P(None, "cells"),
        P("cells"),
        P("cells", None),
        P(None, "waves"),
        P("waves", None),
        P(),
        P(),
        P(),
        P(None, "waves"),
        P("waves", None),
    )
    return jax.shard_map(
        shards, mesh=mesh, in_specs=placed, out_specs=P("cells", "waves"), check_vma=False
    )
```

time: 1160 us -> 195 us (0.17); the launches traced: 1140 us -> 195 us
  waiting for transfers between devices: 619 us -> 0 us
  matrix products: 280 us -> 0 us
  Pallas kernels: 0 us -> 175 us
  blocking collectives: 163 us -> 4.22 us
  other arithmetic: 28.1 us -> 6.67 us
  loops' own time: 15.7 us -> 0 us
  between operations: 15.1 us -> 0.71 us
    psum x1 -> x0, waiting for transfers between devices: 497 us -> none  [shards(): cos_total, sin_total = lax.psum((cos_sum, sin_sum), 'cells')]
    dot_general x18 -> x0, matrix products: 280 us -> none  [the longest x4 73.9 us: add_block(): lax.dot_general(sine_block, sin_part, contract, preferred_element_type=jn...]
    pallas_call x0 -> x5, Pallas kernels: none -> 175 us  [the longest x1 70.6 us: exchange(): pl.pallas_call(exchange_kernel, in_specs=[vmem, hbm, hbm, hbm, vmem, hbm,...]
    psum x1 -> x0, blocking collectives: 163 us -> none  [shards(): count = lax.psum(jnp.sum(occupancy).astype(jnp.float32), 'cells')]
    all_gather x2 -> x0, waiting for transfers between devices: 76 us -> none  [the longest x1 39.8 us: shards(): whole = lax.all_gather(features, 'waves', axis=1, tiled=True)]
    reduce_scatter x2 -> x0, waiting for transfers between devices: 45.1 us -> none  [the longest x1 35.5 us: shards(): lax.psum_scatter(mlp_terms.astype(jnp.bfloat16), 'waves', scatter_dimensi...]
    convert_element_type x4 -> x0, other arithmetic: 18 us -> none  [the longest x1 7.72 us: shards(): sin_filtered = (filters * (sin_total / count_root)).astype(jnp.bfloat16)]
    another operation x2 -> x0, loops' own time: 15.7 us -> none  [the longest x1 15.7 us: shards(): far_sum = lax.fori_loop(0, piece_rows // inner_rows, add_block, empty)]
  transfers between devices with their start and end apart: 9 -> 0, of which waited for: 5 -> 0; matrix products, arithmetic and copies ran while one was open for 2% -> 0% of each run, Pallas kernels for 0% -> 0%
where the time goes in v1:
time: 195 us
  Pallas kernels  175 us (90%)
  local copies, waits for them, and re-layouts  8.68 us (4%)
  other arithmetic  6.67 us (3%)
  blocking collectives  4.22 us (2%)
    pallas_call x1, Pallas kernels, exchange(): pl.pallas_call(exchange_kernel, in_specs=[vmem, hbm, hbm, hbm, vmem, hbm,...  70.6 us
    pallas_call x1, Pallas kernels, forward(): pl.pallas_call(forward_kernel, grid=(K // TILE,), in_specs=[pl.BlockSpec(...  51.3 us
    pallas_call x1, Pallas kernels, mlp(): pl.pallas_call(mlp_kernel, in_specs=[vmem] * 6, out_specs=vmem, out_shape...  27.9 us
    pallas_call x1, Pallas kernels, merge(): pl.pallas_call(merge_kernel, grid=(ROWS // TILE,), in_specs=[pl.BlockSpec...  21.3 us
    all_gather x1, blocking collectives, shards(): whole_waves = lax.all_gather(wavevectors, 'waves', axis=1, tiled=True)  4.22 us

profile of v1, /device:TPU:1, one launch (start us, length us, event | category | flops | bytes accessed | tf_op | source)
XLA Modules:
  0.0 194.8 jit_solution(14671927254490124599)
XLA Ops:
  0.0 0.0 copy-start
  0.0 0.0 copy-start.5
  0.0 0.8 fusion
  0.8 1.5 fusion.1
  2.2 0.0 copy-start.1
  2.3 1.5 copy.16.feats_ref
  3.7 0.0 copy-done.5
  3.7 0.0 copy-start.4
  3.7 0.0 copy-start.7
  3.7 4.2 %all_gather.3.wave_ref = f32[3,4096]{1,0:T(4,128)} all-gather(f32[3,2048]{1,0:T(4,128)S(1)} %copy-done.5), channel_id=1, replica_groups=mesh['cells'=64,'waves'=2] {'waves'}, dimensions={1}, use_global_device_ids=true | all-gather | bytes 73728 | tf_op jit(solution)/shard_map/all_gather | solution.py:495
  7.9 3.5 %shard_map.109 = (bf16[2048,128]{1,0:T(8,128)(2,1)}, bf16[128,4096]{1,0:T(8,128)(2,1)}) custom-call(f32[3,2048]{1,0:T(4,128)} %pos_ref.1, f32[3,4096]{1,0:T(4,128)} %all_gather.3.wave_ref), custom_call_target="tpu_custom_call" | custom-call | tf_op jit(solution)/shard_map/pallas_call | solution.py:76
  11.4 51.3 %shard_map.110 = (bf16[2048,4096]{1,0:T(8,128)(2,1)}, bf16[2048,4096]{1,0:T(8,128)(2,1)}, bf16[2,32,256,128]{3,2,1,0:T(8,128)(2,1)}) custom-call(bf16[2048,128]{1,0:T(8,128)(2,1)} %get-tuple-element.27.left_ref, bf16[128,4096]{1,0:T(8,128)(2,1)} %get-tuple-element.28.right_ref, bf16[256,2048]{1,0:T(8,128)(2,1)} %copy.16.feats_ref), custom_call_target="tpu_custom_call" | custom-call | tf_op jit(solution)/shard_map/pallas_call | solution.py:114
  62.7 0.0 copy-done.1
  62.7 1.2 broadcast_select_fusion.feats_ref
  63.9 0.0 copy-done.4
  63.9 0.6 pad.6.pos_ref
  64.5 0.0 copy-done.7
  64.5 0.7 reduce_sum.9
  65.8 0.6 broadcast_in_dim.21.count_ref
  66.4 0.0 copy-start.8
  66.4 0.0 copy-start.3
  66.4 0.0 copy-start.2
  66.4 70.6 %shard_map.111 = (bf16[2,4,4,2,128,256]{5,4,3,2,1,0:T(8,128)(2,1)}, bf16[512,512]{1,0:T(8,128)(2,1)}, bf16[512,512]{1,0:T(8,128)(2,1)}, bf16[2,256,256]{2,1,0:T(8,128)(2,1)}, f32[2,8,256]{2,1,0:T(8,128)}) custom-call(bf16[2,4,4,2,256,128]{5,4,3,2,1,0:T(8,128)(2,1)} %bitcast.17, f32[2048,512]{1,0:T(8,128)} %filt_ref.1, ...), custom_call_target="tpu_custom_call" | custom-call | tf_op jit(solution)/shard_map/pallas_call | solution.py:321
  137.0 0.0 copy-start.6
  137.1 0.0 copy-done.8
  137.1 0.8 bitcast_add_fusion.1
  137.9 0.0 copy-done.3
  137.9 0.6 pad_maximum_fusion.1.widepos_ref
  138.5 1.0 slice_bitcast_fusion.1
  139.5 0.0 copy-done.2
  139.5 1.1 pad_maximum_fusion.wide_ref
  140.6 0.0 copy-done
  140.6 0.6 constant_dynamic-slice_fusion.mix_ref
  141.2 1.3 copy.17
  142.6 0.0 copy-done.6
  142.6 0.1 copy.15
  142.7 0.7 reshape.54.neigh_ref
  143.3 21.3 %shard_map.112.merged_ref = f32[2048,256]{1,0:T(8,128)} custom-call(s32[48]{0:T(128)} %reshape.54.neigh_ref, f32[4]{0:T(128)} %fall_ref.1, bf16[2048,4096]{1,0:T(8,128)(2,1)} %get-tuple-element.29.cos_ref, bf16[2048,4096]{1,0:T(8,128)(2,1)} %get-tuple-element.30.sin_ref, bf16[8192,256]{1,0:T(8,128)(2,1)} %bitcast.16, bf16[2048,256]{1,0:T(8,128)(2,1)} %feats_ref.1, ...), custom_call_target="tpu_custom_call" | custom-call | tf_op jit(solution)/shard_map/pallas_call | solution.py:390
  164.6 27.9 %shard_map.113 = bf16[2048,256]{1,0:T(8,128)(2,1)} custom-call(f32[2048,256]{1,0:T(8,128)} %shard_map.112.merged_ref, f32[1,512]{1,0:T(1,128)} %bitcast.19, bf16[512,512]{1,0:T(8,128)(2,1)} %in_ref.3, bf16[512,512]{1,0:T(8,128)(2,1)} %get-tuple-element.35.in2_ref, bf16[512,512]{1,0:T(8,128)(2,1)} %out_ref.3, bf16[512,512]{1,0:T(8,128)(2,1)} %get-tuple-element.36.out2_ref), custom_call_target="tpu_custom_call" | custom-call | tf_op jit(solution)/shard_map/pallas_call | solution.py:474
  192.6 2.3 %copy.19 = bf16[2048,256]{1,0:T(8,128)(2,1)} copy(bf16[2048,256]{1,0:T(8,128)(2,1)} %shard_map.113) | data formatting | bytes 2097152
  (1 shorter events, 0.0 us)
Async XLA Ops:
  0.0 140.6 %copy-start = (f32[4,512]{1,0:T(4,128)S(1)}, f32[4,512]{1,0:T(4,128)}, u32[]{:S(2)}) copy-start(f32[4,512]{1,0:T(4,128)} %param.20) | copy-start | bytes 24580
  0.0 3.7 %copy-start.5 = (f32[3,2048]{1,0:T(4,128)S(1)}, f32[3,2048]{1,0:T(4,128)}, u32[]{:S(2)}) copy-start(f32[3,2048]{1,0:T(4,128)} %param.17) | copy-start | bytes 73732
  2.2 60.4 %copy-start.1 = (bf16[2048,256]{1,0:T(8,128)(2,1)S(1)}, bf16[2048,256]{1,0:T(8,128)(2,1)}, u32[]{:S(2)}) copy-start(bf16[2048,256]{1,0:T(8,128)(2,1)} %feats_ref.1) | copy-start | bytes 3145732
  3.7 60.2 %copy-start.4 = (f32[3,2048]{1,0:T(4,128)S(1)}, f32[3,2048]{1,0:T(4,128)}, u32[]{:S(2)}) copy-start(f32[3,2048]{1,0:T(4,128)} %pos_ref.1) | copy-start | bytes 73732
  3.7 60.8 %copy-start.7 = (s32[16]{0:T(128)S(1)}, s32[16]{0:T(128)}, u32[]{:S(2)}) copy-start(s32[16]{0:T(128)} %param.15) | copy-start | bytes 196
  66.4 70.7 %copy-start.8 = (f32[8]{0:T(128)S(1)}, f32[8]{0:T(128)}, u32[]{:S(2)}) copy-start(f32[8]{0:T(128)} %constant.57.clone.1) | copy-start | bytes 100
  66.4 71.5 %copy-start.3 = (f32[8,2048]{1,0:T(8,128)S(1)}, f32[8,2048]{1,0:T(8,128)}, u32[]{:S(2)}) copy-start(f32[8,2048]{1,0:T(8,128)} %pad.6.pos_ref) | copy-start | bytes 196612
  66.4 73.1 %copy-start.2 = (bf16[2048,256]{1,0:T(8,128)(2,1)S(1)}, bf16[2048,256]{1,0:T(8,128)(2,1)}, u32[]{:S(2)}) copy-start(bf16[2048,256]{1,0:T(8,128)(2,1)} %broadcast_select_fusion.feats_ref) | copy-start | bytes 3145732
  137.0 5.5 %copy-start.6 = (s32[16,3]{0,1:T(4,128)S(1)}, s32[16,3]{0,1:T(4,128)}, u32[]{:S(2)}) copy-start(s32[16,3]{0,1:T(4,128)} %param.16) | copy-start | bytes 580

commit v2 on v0

v2 whole, which is shorter than its diff:
```python
import functools
import math

import jax
import jax.numpy as jnp
from jax import lax
from jax.experimental import pallas as pl
from jax.experimental.pallas import tpu as pltpu
from jax.sharding import PartitionSpec as P

F = 512
K = 4096
CAP = 128
HW = 2
NB = 3
G = 4
EPS = 1e-06
WAVES = 2
PART = 256
ROWS = 2048
LOCAL = 16
LENGTH = 1024.0
KP = 64
TILE = 512
TILES = K // TILE
QUARTERS = 4
BLOCK = 32
LANES = 128
HALF = ROWS // 2
BF = jnp.bfloat16
F32 = jnp.float32
MESH = pl.DeviceIdType.MESH
TURN = 1.0 / (2.0 * math.pi)
LOG2E = 1.4426950408889634

SIN = (4.442867900911655, -7.307443330487869, 3.594787161239145, -0.784371485095076)
COS = (1.4142040799995839, -6.977641979004694, 5.715237169770743, -1.7283443233022544)


def params(**more):
    return pltpu.CompilerParams(vmem_limit_bytes=62 << 20, **more)


def split3(v):
    a = v.astype(BF).astype(F32)
    b = (v - a).astype(BF).astype(F32)
    c = ((v - a) - b).astype(BF).astype(F32)
    return a, b, c


def nearest(v):
    return lax.round(v, lax.RoundingMethod.TO_NEAREST_EVEN)


def trig(turns):
    r = turns - nearest(turns)
    s = r * r
    half_sin = r * (SIN[0] + s * (SIN[1] + s * (SIN[2] + s * SIN[3])))
    half_cos = COS[0] + s * (COS[1] + s * (COS[2] + s * COS[3]))
    return (1.0 - half_sin * half_sin).astype(BF), (half_sin * half_cos).astype(BF)


def pieces_of(parts, width):
    row = lax.broadcasted_iota(jnp.int32, (16, width), 0)
    out = jnp.zeros((16, width), F32)
    for n, piece in enumerate(parts):
        out = jnp.where(row == n, jnp.broadcast_to(piece, (16, width)), out)
    return out


def cell_index(z, x, y, core):
    return ((z * 2 + x) * 4 + y) * 2 + core


MESSAGES = 29
COUNTS = 8
PIECES = 4
PIECE = HALF // PIECES


def layer(
    occ_ref, neigh_ref, fall_ref,
    feats_ref, pos_ref, wave_ref, mix_ref, gain_ref, in_ref, out_ref, filt_ref,
    result_ref,
    wide, widepos, waves_all, left, right, cosines, sines, sums,
    r1, r2a, r2b, s2a, s2b, r3a, r3b, s3a, s3b, r4a, r4b, filtered,
    mine, theirs, counts, rcounts, merged, in2, out2,
    outgoing, incoming, back, returned,
    send_sem, recv_sem, csend_sem, crecv_sem, esend_sem, erecv_sem, msend_sem, mrecv_sem,
    local_sem,
):
    cells = lax.axis_index("cells")
    waves = lax.axis_index("waves")
    other = 1 - waves
    z, x, y, core = cells // 16, (cells // 8) % 2, (cells // 2) % 4, cells % 2

    def at(cell):
        return {"cells": cell, "waves": waves}

    def along_y(d):
        return at(cell_index(z, x, lax.rem(y + d, 4), core))

    def along_z(d):
        return at(cell_index(lax.rem(z + d, 4), x, y, core))

    sibling = at(cell_index(z, x, y, 1 - core))
    along_x = at(cell_index(z, 1 - x, y, core))
    above = at(lax.rem(cells + 1, 64))
    below = at(lax.rem(cells + 63, 64))
    partner = {"cells": cells, "waves": other}

    def copy_of(src, dst, sends, receives, n, device):
        return pltpu.make_async_remote_copy(
            src_ref=src, dst_ref=dst, send_sem=sends.at[n], recv_sem=receives.at[n],
            device_id=device, device_id_type=MESH,
        )

    barrier = pltpu.get_barrier_semaphore()
    peers = [sibling, along_x, partner, above, below]
    peers += [along_y(d) for d in (1, 2, 3)] + [along_z(d) for d in (1, 2, 3)]
    for peer in peers:
        pl.semaphore_signal(barrier, inc=1, device_id=peer, device_id_type=MESH)

    for t in range(TILES // 2):
        waves_all[waves * (TILES // 2) + t, 0:3, :] = wave_ref[:, t * TILE : (t + 1) * TILE]
    for c in range(LOCAL):
        widepos[c + HW, 0:3, :] = pos_ref[:, c * CAP : (c + 1) * CAP]
    slot = lax.broadcasted_iota(jnp.int32, (CAP, PART), 0)
    total = jnp.float32(0.0)
    for c in range(LOCAL):
        block = feats_ref[c * CAP : (c + 1) * CAP, :]
        wide[c + HW] = jnp.where(slot < occ_ref[c], block.astype(F32), 0.0).astype(BF)
        total = total + occ_ref[c].astype(F32)
    counts[0] = jnp.full((8, LANES), total)
    pl.semaphore_wait(barrier, len(peers))

    index = y * 8 + z * 2 + x
    own_lanes = pl.ds(pl.multiple_of(waves * PART, PART), PART)
    far_lanes = pl.ds(pl.multiple_of(other * PART, PART), PART)

    def filter_rows(half):
        return pl.ds(pl.multiple_of(half * 1024 + index * BLOCK, BLOCK), BLOCK)

    own_tiles = pl.ds(waves * (TILES // 2), TILES // 2)
    early = [
        (waves_all.at[own_tiles], waves_all.at[own_tiles], partner),
        (filt_ref.at[filter_rows(0), far_lanes], theirs.at[0], partner),
        (filt_ref.at[filter_rows(1), far_lanes], theirs.at[1], partner),
        (widepos.at[pl.ds(HW, HW)], widepos.at[pl.ds(LOCAL + HW, HW)], below),
        (widepos.at[pl.ds(LOCAL, HW)], widepos.at[pl.ds(0, HW)], above),
        (wide.at[pl.ds(HW, HW)], wide.at[pl.ds(LOCAL + HW, HW)], below),
        (wide.at[pl.ds(LOCAL, HW)], wide.at[pl.ds(0, HW)], above),
        (in_ref, in2, partner),
        (out_ref, out2, partner),
    ]
    early = [
        copy_of(src, dst, esend_sem, erecv_sem, n, device)
        for n, (src, dst, device) in enumerate(early)
    ]
    for copy in early:
        copy.start()
    locals_ = [
        pltpu.make_async_copy(
            filt_ref.at[filter_rows(h), own_lanes], mine.at[h], local_sem.at[h]
        )
        for h in range(2)
    ]
    for copy in locals_:
        copy.start()

    first = cells * LOCAL
    cell_of = lax.broadcasted_iota(jnp.int32, (1, ROWS), 1) // CAP
    parts = []
    for p in range(3):
        v = pos_ref[p : p + 1, :]
        if p == 0:
            v = v - (cell_of + first).astype(F32)
        a, b, _ = split3(v)
        parts += [a, a, b, b]
    row = lax.broadcasted_iota(jnp.int32, (16, ROWS), 0)
    hot = (row == lax.broadcasted_iota(jnp.int32, (16, ROWS), 1) // CAP).astype(F32)
    left[...] = jnp.concatenate([pieces_of(parts, ROWS), hot, hot, hot], axis=0).T.astype(BF)
    merged[...] = feats_ref[...].astype(F32)
    early[0].wait()

    def tile(i):
        waves_here = waves_all[i]
        parts = []
        for p in range(3):
            k1, k2, _ = split3(waves_here[p : p + 1, :] * TURN)
            parts += [k1, k2, k1, k2]
        cell = (lax.broadcasted_iota(jnp.int32, (16, TILE), 0) + first).astype(F32)
        whole = cell * (waves_here[0:1, :] * TURN)
        whole = whole - nearest(whole)
        right[...] = jnp.concatenate([pieces_of(parts, TILE), *split3(whole)], axis=0).astype(BF)
        for b in range(ROWS // 512):
            rows = slice(b * 512, (b + 1) * 512)
            turns = jnp.dot(left[rows, :], right[...], preferred_element_type=F32)
            cosine, sine = trig(turns)
            cosines[i, rows, :] = cosine
            sines[i, rows, :] = sine
        atoms = wide[HW : HW + LOCAL].reshape(ROWS, PART)
        q, p = i // 2, i % 2
        for n, held in enumerate((cosines, sines)):
            part = lax.dot_general(
                held[i], atoms, (((0,), (0,)), ((), ())), preferred_element_type=F32
            )
            sums[n, q, pl.ds(2 * p, 2)] = part.astype(BF).reshape(2, 4, 2, BLOCK, PART)

    lane_a, lane_b = pl.ds(0, LANES), pl.ds(LANES, LANES)

    def messages(stage, q):
        base = q * MESSAGES
        out = []

        def add(src, dst, n, device):
            out.append(copy_of(src, dst, send_sem, recv_sem, base + n, device))

        if stage == 1:
            add(sums.at[1 - core, q], r1.at[q], 0, sibling)
        elif stage == 4:
            add(s3a.at[q, 1 - x], r4a.at[q], 13, along_x)
            add(s3b.at[q, 1 - x], r4b.at[q], 14, along_x)
        elif stage == 5:
            piece = filtered.at[core, q, y, z, x]
            add(piece, piece, 15, along_x)
        elif stage == 8:
            piece = filtered.at[core, q]
            add(piece, piece, 28, sibling)
        else:
            for d in (1, 2, 3):
                ty, tz, m = lax.rem(y + d, 4), lax.rem(z + d, 4), d - 1
                if stage == 2:
                    add(sums.at[core, q, ty, :, :, :, lane_a], r2a.at[q, m], 1 + m, along_y(d))
                    add(sums.at[core, q, :, tz, :, :, lane_b], r2b.at[q, m], 4 + m, along_z(d))
                elif stage == 3:
                    add(s2a.at[q, tz], r3a.at[q, m], 7 + m, along_z(d))
                    add(s2b.at[q, ty], r3b.at[q, m], 10 + m, along_y(d))
                elif stage == 6:
                    piece = filtered.at[core, q, y, z, :, :, lane_a]
                    add(piece, piece, 16 + m, along_z(d))
                    piece = filtered.at[core, q, y, z, :, :, lane_b]
                    add(piece, piece, 19 + m, along_y(d))
                elif stage == 7:
                    piece = filtered.at[core, q, y, :, :, :, lane_a]
                    add(piece, piece, 22 + m, along_y(d))
                    piece = filtered.at[core, q, :, z, :, :, lane_b]
                    add(piece, piece, 25 + m, along_z(d))
        return out

    def count_messages(stage):
        def make(src, n, device):
            return copy_of(counts.at[src], rcounts.at[n], csend_sem, crecv_sem, n, device)

        if stage == 1:
            return [make(0, 0, sibling)]
        if stage == 2:
            return [make(1, d, along_y(d)) for d in (1, 2, 3)]
        if stage == 3:
            return [make(2, 3 + d, along_z(d)) for d in (1, 2, 3)]
        return [make(3, 7, along_x)]

    def count_step(stage):
        if stage > 1:
            arrived = count_messages(stage - 1)
            for copy in arrived:
                copy.wait()
            begin = (0, 0, 1, 4, 7)[stage - 1]
            value = counts[stage - 2]
            for n in range(len(arrived)):
                value = value + rcounts[begin + n]
            counts[stage - 1] = value
        if stage < 5:
            for copy in count_messages(stage):
                copy.start()

    def advance(stage, q):
        if stage > 1:
            for copy in messages(stage - 1, q):
                copy.wait()
        if stage <= 5:

            @pl.when(q == 0)
            def _():
                count_step(stage)
                if stage == 5:
                    for copy in early[1:3]:
                        copy.wait()
                    for copy in locals_:
                        copy.wait()

        if stage == 2:

            def add1(n, carry):
                yy, zz = n // 4, n % 4
                sums[core, q, yy, zz] = (
                    sums[core, q, yy, zz].astype(F32) + r1[q, yy, zz].astype(F32)
                ).astype(BF)
                return carry

            lax.fori_loop(0, 16, add1, 0)
        elif stage == 3:
            for p in range(4):
                a = sums[core, q, y, p, :, :, 0:LANES].astype(F32)
                b = sums[core, q, p, z, :, :, LANES:PART].astype(F32)
                for d in range(3):
                    a += r2a[q, d, p].astype(F32)
                    b += r2b[q, d, p].astype(F32)
                s2a[q, p] = a.astype(BF)
                s2b[q, p] = b.astype(BF)
        elif stage == 4:
            a, b = s2a[q, z].astype(F32), s2b[q, y].astype(F32)
            for d in range(3):
                a += r3a[q, d].astype(F32)
                b += r3b[q, d].astype(F32)
            s3a[q] = a.astype(BF)
            s3b[q] = b.astype(BF)
        elif stage == 5:
            root = jnp.sqrt(counts[4][0:1, :])
            here = (q // 2) == waves
            filters = jnp.where(here, mine[q % 2], theirs[q % 2])
            a = s3a[q, x].astype(F32) + r4a[q].astype(F32)
            b = s3b[q, x].astype(F32) + r4b[q].astype(F32)
            filtered[core, q, y, z, x, :, 0:LANES] = (
                filters[:, 0:LANES] * (a / root)
            ).astype(BF)
            filtered[core, q, y, z, x, :, LANES:PART] = (
                filters[:, LANES:PART] * (b / root)
            ).astype(BF)
        if stage < 9:
            for copy in messages(stage, q):
                copy.start()

    def near(c):
        here = widepos[c + HW].T
        sums_ = [jnp.zeros((CAP, PART), F32) for _ in range(G)]
        for n in range(NB):
            place = c + HW + neigh_ref[c * NB + n]
            shift = jnp.where((cells == 0) & (place < HW), -LENGTH, 0.0) + jnp.where(
                (cells == 63) & (place >= LOCAL + HW), LENGTH, 0.0
            )
            there = widepos[place]
            squared = None
            for p in range(3):
                d = here[:, p : p + 1] - (there[p : p + 1, :] + (shift if p == 0 else 0.0))
                squared = d * d if squared is None else squared + d * d
            block = wide[place]
            for g in range(G):
                weight = jnp.exp(-fall_ref[g] * squared).astype(BF)
                sums_[g] += jnp.dot(weight, block, preferred_element_type=F32)
        rows = pl.ds(pl.multiple_of(c * CAP, CAP), CAP)
        value = merged[rows, :]
        for g in range(G):
            value += sums_[g] * mix_ref[g : g + 1, own_lanes]
        merged[rows, :] = value

    scale_far = 1.0 / math.sqrt(K)

    def far(q, rows):
        value = None
        for n, held in enumerate((cosines, sines)):
            factors = filtered[n, q].reshape(2 * TILE, PART)
            for p in range(2):
                term = jnp.dot(
                    held[2 * q + p, rows, :],
                    factors[p * TILE : (p + 1) * TILE],
                    preferred_element_type=F32,
                )
                value = term if value is None else value + term
        return merged[rows, :] + value * scale_far

    def far_block(q, b):
        rows = pl.ds(pl.multiple_of(b * PIECE, PIECE), PIECE)
        merged[rows, :] = far(q, rows)

    def slots(m, carry):
        @pl.when(m < 4)
        def _():
            tile(2 * m)

        @pl.when(m == 4)
        def _():
            for copy in early[3:7]:
                copy.wait()

        @pl.when(m >= 4)
        def _():
            lax.fori_loop(0, 2, lambda j, c: (near((m - 4) * 4 + j), c)[1], 0)

        for stage in (2, 4, 6, 8):
            q = m - stage // 2

            @pl.when((q >= 0) & (q < QUARTERS))
            def _(stage=stage, q=q):
                advance(stage, q)

        @pl.when(m < 4)
        def _():
            tile(2 * m + 1)
            advance(1, m)

        @pl.when(m >= 4)
        def _():
            lax.fori_loop(2, 4, lambda j, c: (near((m - 4) * 4 + j), c)[1], 0)

        for stage in (3, 5, 7, 9):
            q = m - (stage - 1) // 2

            @pl.when((q >= 0) & (q < QUARTERS))
            def _(stage=stage, q=q):
                advance(stage, q)

        @pl.when((m >= 4) & (m < 7))
        def _():
            lax.fori_loop(0, ROWS // PIECE, lambda b, c: (far_block(m - 4, b), c)[1], 0)

        return carry

    lax.fori_loop(0, 8, slots, 0)

    def forth(n):
        return copy_of(outgoing.at[n], incoming.at[n], msend_sem, mrecv_sem, n, partner)

    def home(n):
        return copy_of(back.at[n], returned.at[n], msend_sem, mrecv_sem, PIECES + n, partner)

    def rows_of(side, n):
        return pl.ds(pl.multiple_of(side * HALF + n * PIECE, PIECE), PIECE)

    def give(n, carry):
        rows = rows_of(other, n)
        value = far(QUARTERS - 1, rows)
        merged[rows, :] = value
        outgoing[n] = value.astype(BF)
        forth(n).start()
        return carry

    def keep(n, carry):
        rows = rows_of(waves, n)
        merged[rows, :] = far(QUARTERS - 1, rows)
        return carry

    def mlp(n, carry):
        forth(n).wait()
        rows = rows_of(waves, n)
        own = merged[rows, :]
        their = incoming[n].astype(F32)
        square = jnp.sum(own * own + their * their, axis=1, keepdims=True)
        scale = lax.rsqrt(square * (1.0 / F) + EPS)
        own_n = (own * scale * gain_ref[:, own_lanes]).astype(BF)
        their_n = (their * scale * gain_ref[:, far_lanes]).astype(BF)
        add_own, add_their = own, jnp.zeros_like(own)
        for up, down in ((in_ref, out_ref), (in2, out2)):
            hidden = jnp.dot(
                own_n, up[own_lanes, :], preferred_element_type=F32
            ) + jnp.dot(their_n, up[far_lanes, :], preferred_element_type=F32)
            hidden = (hidden / (1.0 + jnp.exp(-hidden))).astype(BF)
            add_own += jnp.dot(hidden, down[:, own_lanes], preferred_element_type=F32)
            add_their += jnp.dot(hidden, down[:, far_lanes], preferred_element_type=F32)
        back[n] = add_their.astype(BF)
        home(n).start()
        result_ref[rows, :] = add_own.astype(BF)
        return carry

    def finish(n, carry):
        home(n).wait()
        rows = rows_of(other, n)
        result_ref[rows, :] = (merged[rows, :] + returned[n].astype(F32)).astype(BF)
        return carry

    lax.fori_loop(0, PIECES, give, 0)
    lax.fori_loop(0, PIECES, keep, 0)
    for copy in early[7:]:
        copy.wait()
    lax.fori_loop(0, PIECES, mlp, 0)
    lax.fori_loop(0, PIECES, finish, 0)


def shards(
    features, positions, occupancy, neighbours, wavevectors, filters,
    falloffs, mixing, norm_gain, in_weight, out_weight,
):
    smem = pl.BlockSpec(memory_space=pltpu.SMEM)
    vmem = pl.BlockSpec(memory_space=pltpu.VMEM)
    hbm = pl.BlockSpec(memory_space=pl.ANY)
    half = (QUARTERS, 3, 4, 2, BLOCK, LANES)
    return pl.pallas_call(
        layer,
        in_specs=[smem] * 3 + [vmem] * 7 + [hbm],
        out_specs=vmem,
        out_shape=jax.ShapeDtypeStruct((ROWS, PART), BF),
        scratch_shapes=[
            pltpu.VMEM((LOCAL + 2 * HW, CAP, PART), BF),
            pltpu.VMEM((LOCAL + 2 * HW, 8, CAP), F32),
            pltpu.VMEM((TILES, 8, TILE), F32),
            pltpu.VMEM((ROWS, KP), BF),
            pltpu.VMEM((KP, TILE), BF),
            pltpu.VMEM((TILES, ROWS, TILE), BF),
            pltpu.VMEM((TILES, ROWS, TILE), BF),
            pltpu.VMEM((2, QUARTERS, 4, 4, 2, BLOCK, PART), BF),
            pltpu.VMEM((QUARTERS, 4, 4, 2, BLOCK, PART), BF),
            pltpu.VMEM(half, BF),
            pltpu.VMEM(half, BF),
            pltpu.VMEM((QUARTERS, 4, 2, BLOCK, LANES), BF),
            pltpu.VMEM((QUARTERS, 4, 2, BLOCK, LANES), BF),
            pltpu.VMEM((QUARTERS, 3, 2, BLOCK, LANES), BF),
            pltpu.VMEM((QUARTERS, 3, 2, BLOCK, LANES), BF),
            pltpu.VMEM((QUARTERS, 2, BLOCK, LANES), BF),
            pltpu.VMEM((QUARTERS, 2, BLOCK, LANES), BF),
            pltpu.VMEM((QUARTERS, BLOCK, LANES), BF),
            pltpu.VMEM((QUARTERS, BLOCK, LANES), BF),
            pltpu.VMEM((2, QUARTERS, 4, 4, 2, BLOCK, PART), BF),
            pltpu.VMEM((2, BLOCK, PART), F32),
            pltpu.VMEM((2, BLOCK, PART), F32),
            pltpu.VMEM((5, 8, LANES), F32),
            pltpu.VMEM((COUNTS, 8, LANES), F32),
            pltpu.VMEM((ROWS, PART), F32),
            pltpu.VMEM(in_weight.shape, BF),
            pltpu.VMEM(out_weight.shape, BF),
        ]
        + [pltpu.VMEM((PIECES, PIECE, PART), BF)] * 4
        + [pltpu.SemaphoreType.DMA((QUARTERS * MESSAGES,))] * 2
        + [pltpu.SemaphoreType.DMA((COUNTS,))] * 2
        + [pltpu.SemaphoreType.DMA((9,))] * 2
        + [pltpu.SemaphoreType.DMA((2 * PIECES,))] * 2
        + [pltpu.SemaphoreType.DMA((2,))],
        compiler_params=params(collective_id=0, has_side_effects=True),
    )(
        occupancy, neighbours.reshape(LOCAL * NB), falloffs,
        features, positions, wavevectors, mixing, norm_gain[None, :],
        in_weight, out_weight, filters,
    )


def solution(mesh):
    placed = (
        P("cells", "waves"),
        P(None, "cells"),
        P("cells"),
        P("cells", None),
        P(None, "waves"),
        P("waves", None),
        P(),
        P(),
        P(),
        P(None, "waves"),
        P("waves", None),
    )
    return jax.shard_map(
        shards, mesh=mesh, in_specs=placed, out_specs=P("cells", "waves"), check_vma=False
    )
```

time: 1160 us -> 116 us (0.10); the launches traced: 1140 us -> 116 us
  waiting for transfers between devices: 619 us -> 0 us
  matrix products: 280 us -> 0 us
  blocking collectives: 163 us -> 0 us
  Pallas kernels: 0 us -> 112 us
  other arithmetic: 28.1 us -> 0 us
  loops' own time: 15.7 us -> 0 us
  between operations: 15.1 us -> 0.01 us
    psum x1 -> x0, waiting for transfers between devices: 497 us -> none  [shards(): cos_total, sin_total = lax.psum((cos_sum, sin_sum), 'cells')]
    dot_general x18 -> x0, matrix products: 280 us -> none  [the longest x4 73.9 us: add_block(): lax.dot_general(sine_block, sin_part, contract, preferred_element_type=jn...]
    psum x1 -> x0, blocking collectives: 163 us -> none  [shards(): count = lax.psum(jnp.sum(occupancy).astype(jnp.float32), 'cells')]
    pallas_call x0 -> x1, Pallas kernels: none -> 112 us  [shards(): pl.pallas_call(layer, in_specs=[smem] * 3 + [vmem] * 7 + [hbm], out_specs...]
    all_gather x2 -> x0, waiting for transfers between devices: 76 us -> none  [the longest x1 39.8 us: shards(): whole = lax.all_gather(features, 'waves', axis=1, tiled=True)]
    reduce_scatter x2 -> x0, waiting for transfers between devices: 45.1 us -> none  [the longest x1 35.5 us: shards(): lax.psum_scatter(mlp_terms.astype(jnp.bfloat16), 'waves', scatter_dimensi...]
    convert_element_type x4 -> x0, other arithmetic: 18 us -> none  [the longest x1 7.72 us: shards(): sin_filtered = (filters * (sin_total / count_root)).astype(jnp.bfloat16)]
    another operation x2 -> x0, loops' own time: 15.7 us -> none  [the longest x1 15.7 us: shards(): far_sum = lax.fori_loop(0, piece_rows // inner_rows, add_block, empty)]
  transfers between devices with their start and end apart: 9 -> 0, of which waited for: 5 -> 0; matrix products, arithmetic and copies ran while one was open for 2% -> 0% of each run, Pallas kernels for 0% -> 0%
where the time goes in v2:
time: 116 us
  Pallas kernels  112 us (97%)
  local copies, waits for them, and re-layouts  3.62 us (3%)
    pallas_call x1, Pallas kernels, shards(): pl.pallas_call(layer, in_specs=[smem] * 3 + [vmem] * 7 + [hbm], out_specs...  112 us
    unnamed x2, local copies, waits for them, and re-layouts  3.02 us

profile of v2, /device:TPU:1, one launch (start us, length us, event | category | flops | bytes accessed | tf_op | source)
XLA Modules:
  0.0 115.7 jit_solution(11914924644451864712)
XLA Ops:
  0.0 0.8 copy.13
  0.8 0.6 reshape.3.neigh_ref
  1.4 112.1 %shard_map.109 = bf16[2048,256]{1,0:T(8,128)(2,1)} custom-call(s32[16]{0:T(128)} %occ_ref.1, s32[48]{0:T(128)} %reshape.3.neigh_ref, f32[4]{0:T(128)} %fall_ref.1, bf16[2048,256]{1,0:T(8,128)(2,1)} %feats_ref.1, f32[3,2048]{1,0:T(4,128)} %pos_ref.1, f32[3,2048]{1,0:T(4,128)} %wave_ref.1, f32[4,512]{1,0:T(4,128)} %mix_ref.1, f32[1,512]{1,0:T(1,128)} %bitcast.1, ...), custom_call_target="tpu_custom_call" | custom-call | tf_op jit(solution)/shard_map/pallas_call | solution.py:487
  113.5 2.3 %copy.15 = bf16[2048,256]{1,0:T(8,128)(2,1)} copy(bf16[2048,256]{1,0:T(8,128)(2,1)} %shard_map.109) | data formatting | bytes 2097152

commit v3 on v2

--- a/solution.py
+++ b/solution.py
@@ -72,8 +72,9 @@
     return ((z * 2 + x) * 4 + y) * 2 + core
 
 
-MESSAGES = 29
-COUNTS = 8
+MESSAGES = 10
+COUNTS = 11
+STAGES = 7
 PIECES = 4
 PIECE = HALF // PIECES
 
@@ -83,11 +84,11 @@
     feats_ref, pos_ref, wave_ref, mix_ref, gain_ref, in_ref, out_ref, filt_ref,
     result_ref,
     wide, widepos, waves_all, left, right, cosines, sines, sums,
-    r1, r2a, r2b, s2a, s2b, r3a, r3b, s3a, s3b, r4a, r4b, filtered,
-    mine, theirs, counts, rcounts, merged, in2, out2,
+    r1, r2a, r2b, s2a, s2b, r3a, r3b, filtered,
+    mine, theirs, counts, rcounts, merged, weights,
     outgoing, incoming, back, returned,
     send_sem, recv_sem, csend_sem, crecv_sem, esend_sem, erecv_sem, msend_sem, mrecv_sem,
-    local_sem,
+    wsend_sem, wrecv_sem, local_sem,
 ):
     cells = lax.axis_index("cells")
     waves = lax.axis_index("waves")
@@ -103,8 +104,15 @@
     def along_z(d):
         return at(cell_index(lax.rem(z + d, 4), x, y, core))
 
+    def among_zx(d):
+        g = lax.rem(z * 2 + x + d, 8)
+        return g // 2, g % 2, at(cell_index(g // 2, g % 2, y, core))
+
+    def among_yx(d):
+        g = lax.rem(y * 2 + x + d, 8)
+        return g // 2, g % 2, at(cell_index(z, g % 2, g // 2, core))
+
     sibling = at(cell_index(z, x, y, 1 - core))
-    along_x = at(cell_index(z, 1 - x, y, core))
     above = at(lax.rem(cells + 1, 64))
     below = at(lax.rem(cells + 63, 64))
     partner = {"cells": cells, "waves": other}
@@ -116,13 +124,13 @@
         )
 
     barrier = pltpu.get_barrier_semaphore()
-    peers = [sibling, along_x, partner, above, below]
-    peers += [along_y(d) for d in (1, 2, 3)] + [along_z(d) for d in (1, 2, 3)]
+    peers = [sibling, partner, above, below]
+    peers += [among(d)[2] for d in range(1, 8) for among in (among_zx, among_yx)]
     for peer in peers:
         pl.semaphore_signal(barrier, inc=1, device_id=peer, device_id_type=MESH)
 
     for t in range(TILES // 2):
-        waves_all[waves * (TILES // 2) + t, 0:3, :] = wave_ref[:, t * TILE : (t + 1) * TILE]
+        waves_all[t, 0:3, :] = wave_ref[:, t * TILE : (t + 1) * TILE]
     for c in range(LOCAL):
         widepos[c + HW, 0:3, :] = pos_ref[:, c * CAP : (c + 1) * CAP]
     slot = lax.broadcasted_iota(jnp.int32, (CAP, PART), 0)
@@ -132,7 +140,6 @@
         wide[c + HW] = jnp.where(slot < occ_ref[c], block.astype(F32), 0.0).astype(BF)
         total = total + occ_ref[c].astype(F32)
     counts[0] = jnp.full((8, LANES), total)
-    pl.semaphore_wait(barrier, len(peers))
 
     index = y * 8 + z * 2 + x
     own_lanes = pl.ds(pl.multiple_of(waves * PART, PART), PART)
@@ -141,24 +148,20 @@
     def filter_rows(half):
         return pl.ds(pl.multiple_of(half * 1024 + index * BLOCK, BLOCK), BLOCK)
 
-    own_tiles = pl.ds(waves * (TILES // 2), TILES // 2)
+    own_tiles, far_tiles = pl.ds(0, TILES // 2), pl.ds(TILES // 2, TILES // 2)
     early = [
-        (waves_all.at[own_tiles], waves_all.at[own_tiles], partner),
+        (waves_all.at[own_tiles], waves_all.at[far_tiles], partner),
         (filt_ref.at[filter_rows(0), far_lanes], theirs.at[0], partner),
         (filt_ref.at[filter_rows(1), far_lanes], theirs.at[1], partner),
         (widepos.at[pl.ds(HW, HW)], widepos.at[pl.ds(LOCAL + HW, HW)], below),
         (widepos.at[pl.ds(LOCAL, HW)], widepos.at[pl.ds(0, HW)], above),
         (wide.at[pl.ds(HW, HW)], wide.at[pl.ds(LOCAL + HW, HW)], below),
         (wide.at[pl.ds(LOCAL, HW)], wide.at[pl.ds(0, HW)], above),
-        (in_ref, in2, partner),
-        (out_ref, out2, partner),
     ]
     early = [
         copy_of(src, dst, esend_sem, erecv_sem, n, device)
         for n, (src, dst, device) in enumerate(early)
     ]
-    for copy in early:
-        copy.start()
     locals_ = [
         pltpu.make_async_copy(
             filt_ref.at[filter_rows(h), own_lanes], mine.at[h], local_sem.at[h]
@@ -181,7 +184,6 @@
     hot = (row == lax.broadcasted_iota(jnp.int32, (16, ROWS), 1) // CAP).astype(F32)
     left[...] = jnp.concatenate([pieces_of(parts, ROWS), hot, hot, hot], axis=0).T.astype(BF)
     merged[...] = feats_ref[...].astype(F32)
-    early[0].wait()
 
     def tile(i):
         waves_here = waves_all[i]
@@ -218,35 +220,46 @@
 
         if stage == 1:
             add(sums.at[1 - core, q], r1.at[q], 0, sibling)
-        elif stage == 4:
-            add(s3a.at[q, 1 - x], r4a.at[q], 13, along_x)
-            add(s3b.at[q, 1 - x], r4b.at[q], 14, along_x)
-        elif stage == 5:
-            piece = filtered.at[core, q, y, z, x]
-            add(piece, piece, 15, along_x)
-        elif stage == 8:
+        elif stage == 6:
             piece = filtered.at[core, q]
-            add(piece, piece, 28, sibling)
-        else:
+            add(piece, piece, 1, sibling)
+        elif stage in (2, 5):
             for d in (1, 2, 3):
                 ty, tz, m = lax.rem(y + d, 4), lax.rem(z + d, 4), d - 1
                 if stage == 2:
-                    add(sums.at[core, q, ty, :, :, :, lane_a], r2a.at[q, m], 1 + m, along_y(d))
-                    add(sums.at[core, q, :, tz, :, :, lane_b], r2b.at[q, m], 4 + m, along_z(d))
-                elif stage == 3:
-                    add(s2a.at[q, tz], r3a.at[q, m], 7 + m, along_z(d))
-                    add(s2b.at[q, ty], r3b.at[q, m], 10 + m, along_y(d))
-                elif stage == 6:
-                    piece = filtered.at[core, q, y, z, :, :, lane_a]
-                    add(piece, piece, 16 + m, along_z(d))
-                    piece = filtered.at[core, q, y, z, :, :, lane_b]
-                    add(piece, piece, 19 + m, along_y(d))
-                elif stage == 7:
+                    add(sums.at[core, q, ty, :, :, :, lane_a], r2a.at[q, m], 2, along_y(d))
+                    add(sums.at[core, q, :, tz, :, :, lane_b], r2b.at[q, m], 3, along_z(d))
+                else:
                     piece = filtered.at[core, q, y, :, :, :, lane_a]
-                    add(piece, piece, 22 + m, along_y(d))
+                    add(piece, piece, 4, along_y(d))
                     piece = filtered.at[core, q, :, z, :, :, lane_b]
-                    add(piece, piece, 25 + m, along_z(d))
+                    add(piece, piece, 5, along_z(d))
+        else:
+            for d in range(1, 8):
+                m = d - 1
+                if stage == 3:
+                    tz, tx, device = among_zx(d)
+                    add(s2a.at[q, tz, tx], r3a.at[q, m], 6, device)
+                    ty, tx, device = among_yx(d)
+                    add(s2b.at[q, ty, tx], r3b.at[q, m], 7, device)
+                else:
+                    piece = filtered.at[core, q, y, z, x, :, lane_a]
+                    add(piece, piece, 8, among_zx(d)[2])
+                    piece = filtered.at[core, q, y, z, x, :, lane_b]
+                    add(piece, piece, 9, among_yx(d)[2])
         return out
+
+    def arrivals(stage, q):
+        if stage in (1, 6):
+            return messages(stage, q)
+        first, a, b = {2: (2, r2a, r2b), 3: (6, r3a, r3b), 4: (8, r3a, r3b), 5: (4, r2a, r2b)}[stage]
+        return [
+            copy_of(
+                held.at[q], held.at[q], send_sem, recv_sem,
+                q * MESSAGES + first + n, sibling,
+            )
+            for n, held in enumerate((a, b))
+        ]
 
     def count_messages(stage):
         def make(src, n, device):
@@ -256,34 +269,32 @@
             return [make(0, 0, sibling)]
         if stage == 2:
             return [make(1, d, along_y(d)) for d in (1, 2, 3)]
-        if stage == 3:
-            return [make(2, 3 + d, along_z(d)) for d in (1, 2, 3)]
-        return [make(3, 7, along_x)]
+        return [make(2, 3 + d, among_zx(d)[2]) for d in range(1, 8)]
 
     def count_step(stage):
         if stage > 1:
             arrived = count_messages(stage - 1)
             for copy in arrived:
                 copy.wait()
-            begin = (0, 0, 1, 4, 7)[stage - 1]
+            begin = (0, 0, 1, 4)[stage - 1]
             value = counts[stage - 2]
             for n in range(len(arrived)):
                 value = value + rcounts[begin + n]
             counts[stage - 1] = value
-        if stage < 5:
+        if stage < 4:
             for copy in count_messages(stage):
                 copy.start()
 
     def advance(stage, q):
         if stage > 1:
-            for copy in messages(stage - 1, q):
+            for copy in arrivals(stage - 1, q):
                 copy.wait()
-        if stage <= 5:
+        if stage <= 4:
 
             @pl.when(q == 0)
             def _():
                 count_step(stage)
-                if stage == 5:
+                if stage == 4:
                     for copy in early[1:3]:
                         copy.wait()
                     for copy in locals_:
@@ -309,25 +320,19 @@
                 s2a[q, p] = a.astype(BF)
                 s2b[q, p] = b.astype(BF)
         elif stage == 4:
-            a, b = s2a[q, z].astype(F32), s2b[q, y].astype(F32)
-            for d in range(3):
+            root = jnp.sqrt(counts[3][0:1, :])
+            filters = jnp.where(q < QUARTERS // 2, mine[q % 2], theirs[q % 2])
+            a, b = s2a[q, z, x].astype(F32), s2b[q, y, x].astype(F32)
+            for d in range(7):
                 a += r3a[q, d].astype(F32)
                 b += r3b[q, d].astype(F32)
-            s3a[q] = a.astype(BF)
-            s3b[q] = b.astype(BF)
-        elif stage == 5:
-            root = jnp.sqrt(counts[4][0:1, :])
-            here = (q // 2) == waves
-            filters = jnp.where(here, mine[q % 2], theirs[q % 2])
-            a = s3a[q, x].astype(F32) + r4a[q].astype(F32)
-            b = s3b[q, x].astype(F32) + r4b[q].astype(F32)
             filtered[core, q, y, z, x, :, 0:LANES] = (
                 filters[:, 0:LANES] * (a / root)
             ).astype(BF)
             filtered[core, q, y, z, x, :, LANES:PART] = (
                 filters[:, LANES:PART] * (b / root)
             ).astype(BF)
-        if stage < 9:
+        if stage < STAGES:
             for copy in messages(stage, q):
                 copy.start()
 
@@ -373,50 +378,71 @@
         rows = pl.ds(pl.multiple_of(b * PIECE, PIECE), PIECE)
         merged[rows, :] = far(q, rows)
 
-    def slots(m, carry):
-        @pl.when(m < 4)
+    strip = F // TILES
+
+    def fetch(n, held):
+        rows = pl.ds(pl.multiple_of(n * strip, strip), strip)
+        return copy_of(
+            held.at[rows], weights.at[core, rows], wsend_sem, wrecv_sem, n, partner
+        )
+
+    def hand_over():
+        return copy_of(
+            weights.at[core], weights.at[core], wsend_sem, wrecv_sem, TILES, sibling
+        )
+
+    def slots(n, carry):
+        @pl.when(n == TILES // 2)
         def _():
-            tile(2 * m)
-
-        @pl.when(m == 4)
+            early[0].wait()
+
+        @pl.when(n < TILES)
+        def _():
+            tile(n)
+
+        @pl.when(n == TILES)
         def _():
             for copy in early[3:7]:
                 copy.wait()
 
-        @pl.when(m >= 4)
+        @pl.when(n == TILES + 1)
         def _():
-            lax.fori_loop(0, 2, lambda j, c: (near((m - 4) * 4 + j), c)[1], 0)
-
-        for stage in (2, 4, 6, 8):
-            q = m - stage // 2
-
-            @pl.when((q >= 0) & (q < QUARTERS))
+            for piece in range(TILES):
+                fetch(piece, in_ref).wait()
+            hand_over().start()
+
+        @pl.when(n >= TILES)
+        def _():
+            h = n - TILES
+            begin = 3 * h - jnp.maximum(h - 4, 0)
+            end = jnp.minimum(begin + 3 - h // 4, LOCAL)
+            lax.fori_loop(begin, end, lambda c, carry: (near(c), carry)[1], 0)
+
+        for stage in range(1, STAGES + 1):
+            q = (n - stage) // 2
+
+            @pl.when((n >= stage) & ((n - stage) % 2 == 0) & (n < stage + 2 * QUARTERS))
             def _(stage=stage, q=q):
                 advance(stage, q)
 
-        @pl.when(m < 4)
+        for held, side in ((in_ref, 0), (out_ref, 1)):
+
+            @pl.when((n <= TILES) & (core == side))
+            def _(held=held):
+                fetch(n - 1, held).start()
+
+        @pl.when((n >= STAGES) & ((n - STAGES) % 2 == 0) & (n < STAGES + 2 * QUARTERS - 2))
         def _():
-            tile(2 * m + 1)
-            advance(1, m)
-
-        @pl.when(m >= 4)
-        def _():
-            lax.fori_loop(2, 4, lambda j, c: (near((m - 4) * 4 + j), c)[1], 0)
-
-        for stage in (3, 5, 7, 9):
-            q = m - (stage - 1) // 2
-
-            @pl.when((q >= 0) & (q < QUARTERS))
-            def _(stage=stage, q=q):
-                advance(stage, q)
-
-        @pl.when((m >= 4) & (m < 7))
-        def _():
-            lax.fori_loop(0, ROWS // PIECE, lambda b, c: (far_block(m - 4, b), c)[1], 0)
+            q = (n - STAGES) // 2
+            lax.fori_loop(0, ROWS // PIECE, lambda b, c: (far_block(q, b), c)[1], 0)
 
         return carry
 
-    lax.fori_loop(0, 8, slots, 0)
+    tile(0)
+    pl.semaphore_wait(barrier, len(peers))
+    for copy in early:
+        copy.start()
+    lax.fori_loop(1, STAGES + 2 * QUARTERS - 1, slots, 0)
 
     def forth(n):
         return copy_of(outgoing.at[n], incoming.at[n], msend_sem, mrecv_sem, n, partner)
@@ -450,7 +476,7 @@
         own_n = (own * scale * gain_ref[:, own_lanes]).astype(BF)
         their_n = (their * scale * gain_ref[:, far_lanes]).astype(BF)
         add_own, add_their = own, jnp.zeros_like(own)
-        for up, down in ((in_ref, out_ref), (in2, out2)):
+        for up, down in ((in_ref, out_ref), (weights.at[0], weights.at[1])):
             hidden = jnp.dot(
                 own_n, up[own_lanes, :], preferred_element_type=F32
             ) + jnp.dot(their_n, up[far_lanes, :], preferred_element_type=F32)
@@ -470,8 +496,7 @@
 
     lax.fori_loop(0, PIECES, give, 0)
     lax.fori_loop(0, PIECES, keep, 0)
-    for copy in early[7:]:
-        copy.wait()
+    hand_over().wait()
     lax.fori_loop(0, PIECES, mlp, 0)
     lax.fori_loop(0, PIECES, finish, 0)
 
@@ -503,26 +528,22 @@
             pltpu.VMEM(half, BF),
             pltpu.VMEM((QUARTERS, 4, 2, BLOCK, LANES), BF),
             pltpu.VMEM((QUARTERS, 4, 2, BLOCK, LANES), BF),
-            pltpu.VMEM((QUARTERS, 3, 2, BLOCK, LANES), BF),
-            pltpu.VMEM((QUARTERS, 3, 2, BLOCK, LANES), BF),
-            pltpu.VMEM((QUARTERS, 2, BLOCK, LANES), BF),
-            pltpu.VMEM((QUARTERS, 2, BLOCK, LANES), BF),
-            pltpu.VMEM((QUARTERS, BLOCK, LANES), BF),
-            pltpu.VMEM((QUARTERS, BLOCK, LANES), BF),
+            pltpu.VMEM((QUARTERS, 7, BLOCK, LANES), BF),
+            pltpu.VMEM((QUARTERS, 7, BLOCK, LANES), BF),
             pltpu.VMEM((2, QUARTERS, 4, 4, 2, BLOCK, PART), BF),
             pltpu.VMEM((2, BLOCK, PART), F32),
             pltpu.VMEM((2, BLOCK, PART), F32),
-            pltpu.VMEM((5, 8, LANES), F32),
+            pltpu.VMEM((4, 8, LANES), F32),
             pltpu.VMEM((COUNTS, 8, LANES), F32),
             pltpu.VMEM((ROWS, PART), F32),
-            pltpu.VMEM(in_weight.shape, BF),
-            pltpu.VMEM(out_weight.shape, BF),
+            pltpu.VMEM((2, *in_weight.shape), BF),
         ]
         + [pltpu.VMEM((PIECES, PIECE, PART), BF)] * 4
         + [pltpu.SemaphoreType.DMA((QUARTERS * MESSAGES,))] * 2
         + [pltpu.SemaphoreType.DMA((COUNTS,))] * 2
-        + [pltpu.SemaphoreType.DMA((9,))] * 2
+        + [pltpu.SemaphoreType.DMA((7,))] * 2
         + [pltpu.SemaphoreType.DMA((2 * PIECES,))] * 2
+        + [pltpu.SemaphoreType.DMA((TILES + 1,))] * 2
         + [pltpu.SemaphoreType.DMA((2,))],
         compiler_params=params(collective_id=0, has_side_effects=True),
     )(

time: 116 us -> 105 us (0.905)
  Pallas kernels: 112 us -> 101 us
    pallas_call x1, Pallas kernels: 112 us -> 101 us  [shards(): pl.pallas_call(layer, in_specs=[smem] * 3 + [vmem] * 7 + [hbm], out_specs...]
where the time goes in v3:
time: 105 us
  Pallas kernels  101 us (96%)
  local copies, waits for them, and re-layouts  3.62 us (3%)
    pallas_call x1, Pallas kernels, shards(): pl.pallas_call(layer, in_specs=[smem] * 3 + [vmem] * 7 + [hbm], out_specs...  101 us
    unnamed x2, local copies, waits for them, and re-layouts  3.02 us

profile of v3, /device:TPU:1, one launch (start us, length us, event | category | flops | bytes accessed | tf_op | source)
XLA Modules:
  0.0 104.7 jit_solution(13987408972816814272)
XLA Ops:
  0.0 0.8 copy.13
  0.8 0.6 reshape.3.neigh_ref
  1.4 101.1 %shard_map.109 = bf16[2048,256]{1,0:T(8,128)(2,1)} custom-call(s32[16]{0:T(128)} %occ_ref.1, s32[48]{0:T(128)} %reshape.3.neigh_ref, f32[4]{0:T(128)} %fall_ref.1, bf16[2048,256]{1,0:T(8,128)(2,1)} %feats_ref.1, f32[3,2048]{1,0:T(4,128)} %pos_ref.1, f32[3,2048]{1,0:T(4,128)} %wave_ref.1, f32[4,512]{1,0:T(4,128)} %mix_ref.1, f32[1,512]{1,0:T(1,128)} %bitcast.1, ...), custom_call_target="tpu_custom_call" | custom-call | tf_op jit(solution)/shard_map/pallas_call | solution.py:512
  102.4 2.3 %copy.15 = bf16[2048,256]{1,0:T(8,128)(2,1)} copy(bf16[2048,256]{1,0:T(8,128)(2,1)} %shard_map.109) | data formatting | bytes 2097152

commit v4 on v3

--- a/solution.py
+++ b/solution.py
@@ -86,7 +86,7 @@
     wide, widepos, waves_all, left, right, cosines, sines, sums,
     r1, r2a, r2b, s2a, s2b, r3a, r3b, filtered,
     mine, theirs, counts, rcounts, merged, weights,
-    outgoing, incoming, back, returned,
+    outgoing, incoming, returned,
     send_sem, recv_sem, csend_sem, crecv_sem, esend_sem, erecv_sem, msend_sem, mrecv_sem,
     wsend_sem, wrecv_sem, local_sem,
 ):
@@ -391,6 +391,23 @@
             weights.at[core], weights.at[core], wsend_sem, wrecv_sem, TILES, sibling
         )
 
+    reached = (
+        (1, 3, 5, 7), (2, 4, 6, 8), (4, 6, 8, 9), (6, 8, 9, 10),
+        (8, 9, 10, 11), (9, 10, 11, 12), (10, 11, 12, 13),
+    )
+
+    def chunk_at(n, choices):
+        q = jnp.int32(0)
+        for choice in choices[:-1]:
+            q = q + jnp.where(n > choice, 1, 0)
+        return q
+
+    def any_of(value, choices):
+        found = value == choices[0]
+        for choice in choices[1:]:
+            found = found | (value == choice)
+        return found
+
     def slots(n, carry):
         @pl.when(n == TILES // 2)
         def _():
@@ -399,6 +416,12 @@
         @pl.when(n < TILES)
         def _():
             tile(n)
+
+        @pl.when(n == 0)
+        def _():
+            pl.semaphore_wait(barrier, len(peers))
+            for copy in early:
+                copy.start()
 
         @pl.when(n == TILES)
         def _():
@@ -419,36 +442,32 @@
             lax.fori_loop(begin, end, lambda c, carry: (near(c), carry)[1], 0)
 
         for stage in range(1, STAGES + 1):
-            q = (n - stage) // 2
-
-            @pl.when((n >= stage) & ((n - stage) % 2 == 0) & (n < stage + 2 * QUARTERS))
-            def _(stage=stage, q=q):
+            slots_of = reached[stage - 1]
+
+            @pl.when(any_of(n, slots_of))
+            def _(stage=stage, q=chunk_at(n, slots_of)):
                 advance(stage, q)
 
         for held, side in ((in_ref, 0), (out_ref, 1)):
 
-            @pl.when((n <= TILES) & (core == side))
+            @pl.when((n >= 1) & (n <= TILES) & (core == side))
             def _(held=held):
                 fetch(n - 1, held).start()
 
-        @pl.when((n >= STAGES) & ((n - STAGES) % 2 == 0) & (n < STAGES + 2 * QUARTERS - 2))
-        def _():
-            q = (n - STAGES) // 2
+        @pl.when(any_of(n, reached[-1][:-1]))
+        def _():
+            q = chunk_at(n, reached[-1])
             lax.fori_loop(0, ROWS // PIECE, lambda b, c: (far_block(q, b), c)[1], 0)
 
         return carry
 
-    tile(0)
-    pl.semaphore_wait(barrier, len(peers))
-    for copy in early:
-        copy.start()
-    lax.fori_loop(1, STAGES + 2 * QUARTERS - 1, slots, 0)
+    lax.fori_loop(0, STAGES + 2 * QUARTERS - 1, slots, 0)
 
     def forth(n):
         return copy_of(outgoing.at[n], incoming.at[n], msend_sem, mrecv_sem, n, partner)
 
     def home(n):
-        return copy_of(back.at[n], returned.at[n], msend_sem, mrecv_sem, PIECES + n, partner)
+        return copy_of(outgoing.at[n], returned.at[n], msend_sem, mrecv_sem, PIECES + n, partner)
 
     def rows_of(side, n):
         return pl.ds(pl.multiple_of(side * HALF + n * PIECE, PIECE), PIECE)
@@ -483,7 +502,7 @@
             hidden = (hidden / (1.0 + jnp.exp(-hidden))).astype(BF)
             add_own += jnp.dot(hidden, down[:, own_lanes], preferred_element_type=F32)
             add_their += jnp.dot(hidden, down[:, far_lanes], preferred_element_type=F32)
-        back[n] = add_their.astype(BF)
+        outgoing[n] = add_their.astype(BF)
         home(n).start()
         result_ref[rows, :] = add_own.astype(BF)
         return carry
@@ -538,7 +557,7 @@
             pltpu.VMEM((ROWS, PART), F32),
             pltpu.VMEM((2, *in_weight.shape), BF),
         ]
-        + [pltpu.VMEM((PIECES, PIECE, PART), BF)] * 4
+        + [pltpu.VMEM((PIECES, PIECE, PART), BF)] * 3
         + [pltpu.SemaphoreType.DMA((QUARTERS * MESSAGES,))] * 2
         + [pltpu.SemaphoreType.DMA((COUNTS,))] * 2
         + [pltpu.SemaphoreType.DMA((7,))] * 2

time: 105 us -> 102 us (0.971); the launches traced: 105 us -> 100 us
  Pallas kernels: 101 us -> 96.3 us
    pallas_call x1, Pallas kernels: 101 us -> 96.3 us  [shards(): pl.pallas_call(layer, in_specs=[smem] * 3 + [vmem] * 7 + [hbm], out_specs...]
where the time goes in v4:
time: 102 us; the launch traced here: 100 us
  Pallas kernels  96.3 us (94%)
  local copies, waits for them, and re-layouts  3.62 us (4%)
    pallas_call x1, Pallas kernels, shards(): pl.pallas_call(layer, in_specs=[smem] * 3 + [vmem] * 7 + [hbm], out_specs...  96.3 us
    unnamed x2, local copies, waits for them, and re-layouts  3.02 us

profile of v4, /device:TPU:1, one launch (start us, length us, event | category | flops | bytes accessed | tf_op | source)
XLA Modules:
  0.0 100.0 jit_solution(15094713018086821332)
XLA Ops:
  0.0 0.8 copy.13
  0.8 0.6 reshape.3.neigh_ref
  1.4 96.3 %shard_map.109 = bf16[2048,256]{1,0:T(8,128)(2,1)} custom-call(s32[16]{0:T(128)} %occ_ref.1, s32[48]{0:T(128)} %reshape.3.neigh_ref, f32[4]{0:T(128)} %fall_ref.1, bf16[2048,256]{1,0:T(8,128)(2,1)} %feats_ref.1, f32[3,2048]{1,0:T(4,128)} %pos_ref.1, f32[3,2048]{1,0:T(4,128)} %wave_ref.1, f32[4,512]{1,0:T(4,128)} %mix_ref.1, f32[1,512]{1,0:T(1,128)} %bitcast.1, ...), custom_call_target="tpu_custom_call" | custom-call | tf_op jit(solution)/shard_map/pallas_call | solution.py:531
  97.7 2.3 %copy.15 = bf16[2048,256]{1,0:T(8,128)(2,1)} copy(bf16[2048,256]{1,0:T(8,128)(2,1)} %shard_map.109) | data formatting | bytes 2097152

commit v5 on v4

--- a/solution.py
+++ b/solution.py
@@ -38,7 +38,7 @@
 
 
 def params(**more):
-    return pltpu.CompilerParams(vmem_limit_bytes=62 << 20, **more)
+    return pltpu.CompilerParams(vmem_limit_bytes=65400 << 10, **more)
 
 
 def split3(v):
@@ -195,18 +195,23 @@
         whole = cell * (waves_here[0:1, :] * TURN)
         whole = whole - nearest(whole)
         right[...] = jnp.concatenate([pieces_of(parts, TILE), *split3(whole)], axis=0).astype(BF)
-        for b in range(ROWS // 512):
-            rows = slice(b * 512, (b + 1) * 512)
-            turns = jnp.dot(left[rows, :], right[...], preferred_element_type=F32)
-            cosine, sine = trig(turns)
-            cosines[i, rows, :] = cosine
-            sines[i, rows, :] = sine
-        atoms = wide[HW : HW + LOCAL].reshape(ROWS, PART)
+        totals = [None, None]
+        values = None
+        for b in range(ROWS // HALF + 1):
+            if b > 0:
+                atoms = wide[HW + (b - 1) * 8 : HW + b * 8].reshape(HALF, PART)
+                for n, value in enumerate(values):
+                    part = lax.dot_general(
+                        value, atoms, (((0,), (0,)), ((), ())), preferred_element_type=F32
+                    )
+                    totals[n] = part if totals[n] is None else totals[n] + part
+            if b < ROWS // HALF:
+                rows = slice(b * HALF, (b + 1) * HALF)
+                turns = jnp.dot(left[rows, :], right[...], preferred_element_type=F32)
+                values = trig(turns)
+                cosines[i, rows, :], sines[i, rows, :] = values
         q, p = i // 2, i % 2
-        for n, held in enumerate((cosines, sines)):
-            part = lax.dot_general(
-                held[i], atoms, (((0,), (0,)), ((), ())), preferred_element_type=F32
-            )
+        for n, part in enumerate(totals):
             sums[n, q, pl.ds(2 * p, 2)] = part.astype(BF).reshape(2, 4, 2, BLOCK, PART)
 
     lane_a, lane_b = pl.ds(0, LANES), pl.ds(LANES, LANES)

time: 102 us -> 99.6 us (0.976)
  Pallas kernels: 96.3 us -> 94.4 us
    pallas_call x1, Pallas kernels: 96.3 us -> 94.4 us  [shards(): pl.pallas_call(layer, in_specs=[smem] * 3 + [vmem] * 7 + [hbm], out_specs...]
where the time goes in v5:
time: 99.6 us; the launch traced here: 98 us
  Pallas kernels  94.4 us (95%)
  local copies, waits for them, and re-layouts  3.62 us (4%)
    pallas_call x1, Pallas kernels, shards(): pl.pallas_call(layer, in_specs=[smem] * 3 + [vmem] * 7 + [hbm], out_specs...  94.4 us
    unnamed x2, local copies, waits for them, and re-layouts  3.02 us

profile of v5, /device:TPU:1, one launch (start us, length us, event | category | flops | bytes accessed | tf_op | source)
XLA Modules:
  0.0 98.0 jit_solution(5954962987875038217)
XLA Ops:
  0.0 0.8 copy.13
  0.8 0.6 reshape.3.neigh_ref
  1.4 94.4 %shard_map.109 = bf16[2048,256]{1,0:T(8,128)(2,1)} custom-call(s32[16]{0:T(128)} %occ_ref.1, s32[48]{0:T(128)} %reshape.3.neigh_ref, f32[4]{0:T(128)} %fall_ref.1, bf16[2048,256]{1,0:T(8,128)(2,1)} %feats_ref.1, f32[3,2048]{1,0:T(4,128)} %pos_ref.1, f32[3,2048]{1,0:T(4,128)} %wave_ref.1, f32[4,512]{1,0:T(4,128)} %mix_ref.1, f32[1,512]{1,0:T(1,128)} %bitcast.1, ...), custom_call_target="tpu_custom_call" | custom-call | tf_op jit(solution)/shard_map/pallas_call | solution.py:536
  95.8 2.3 %copy.15 = bf16[2048,256]{1,0:T(8,128)(2,1)} copy(bf16[2048,256]{1,0:T(8,128)(2,1)} %shard_map.109) | data formatting | bytes 2097152
